TPU v7x, 32 devices: a whole 2x2x4 slice. The times are simulated.
32 devices in a mesh: tag: 8 (over z, x), tile: 4 (over y, core).
Axes of the slice: x: 2, y: 2, z: 4, core: 2. Of those that a mesh axis runs over, the one named last changes fastest.
Arguments:
- species_slot: int32 [16], replicated, may hold values from 0 to 15, each once
- bulk: float32 [16, 8, 128, 128], P('tag', None, 'tile'), may hold values from 0.3 to 3
- winds: float32 [3, 8, 128, 128], P(None, None, 'tile'), may hold values from -0.35 to 0.35
- fractions: bfloat16 [2, 128, 8, 128, 128], P(None, 'tag', None, 'tile'), may hold values from 0 to 1
Outputs:
- tagged: bfloat16 [2, 128, 8, 128, 128], P(None, 'tag', None, 'tile')
Inputs may be any that keep to these rules, and one draw needn't show every extreme that they name: `species_slot`: every slot appears once; slot v is held by tag group v // 2.
All inputs are finite; a program needn't handle non-finite values.
Results may differ from a plain program's by a relative error of at most 0.0035.
Values may be sent and summed in bfloat16 or wider, within the bound.
No kernel may reach another device: no remote copies, remote signals or barrier semaphores. Data moves between devices by JAX's collectives and lax.ppermute only.
A program may use at most 64 MiB of HBM per device.

v0:
```python
import jax
import jax.numpy as jnp
from jax import lax
from jax.sharding import PartitionSpec as P


def extended(block, sides, width):
    for axis, dim in sides:
        count = lax.axis_size(axis)
        forward = [(i, i + 1) for i in range(count - 1)]
        backward = [(target, source) for source, target in forward]
        low = lax.ppermute(
            lax.slice_in_dim(block, block.shape[dim] - width, None, axis=dim), axis, forward
        )
        high = lax.ppermute(lax.slice_in_dim(block, 0, width, axis=dim), axis, backward)
        block = jnp.concatenate([low, block, high], axis=dim)
    return block


def shifted(value, axis, steps):
    count = lax.axis_size(axis)
    first, last = (max(0, -steps), min(count, count - steps))
    return lax.ppermute(value, axis, [(source, source + steps) for source in range(first, last)])


def broadcast(block, axis, holder):
    block = jnp.where(lax.axis_index(axis) == holder, block, jnp.zeros_like(block))
    return lax.psum(block, axis)


def limited(before_two, before, after, after_two):
    centred = (7.0 * (before + after) - (before_two + after_two)) / 12.0
    return jnp.minimum(jnp.maximum(centred, jnp.minimum(before, after)), jnp.maximum(before, after))


def padded_along(values, along, lower, upper):
    widths = [(0, 0)] * values.ndim
    widths[along] = (lower, upper)
    return jnp.pad(values, widths)


def face_fluxes(cells, courant, along):
    length = cells.shape[along]
    padded = padded_along(cells, along, 2, 1)
    pieces = [lax.slice_in_dim(padded, offset, offset + length, axis=along) for offset in range(4)]
    faces = courant * limited(pieces[0], pieces[1], pieces[2], pieces[3])
    position = lax.broadcasted_iota(jnp.int32, faces.shape, along)
    return jnp.where(position == 0, 0.0, faces)


def tag_divergence(shares, faces, along):
    length = shares.shape[along]
    lower = lax.slice_in_dim(padded_along(shares, along, 1, 0), 0, length, axis=along)
    carried = jnp.maximum(faces, 0.0) * lower + jnp.minimum(faces, 0.0) * shares
    upper = padded_along(lax.slice_in_dim(carried, 1, length, axis=along), along, 0, 1)
    return upper - carried


def rimmed(cells):
    return extended(cells.astype(jnp.bfloat16), (("tile", 1),), 2).astype(cells.dtype)


def all_fluxes(cells, cell_edge, wind_faces, winds, tile_start):
    columns = cells.shape[1]
    first = cell_edge[:, 0 : columns + 1]
    second = cell_edge[:, 1 : columns + 2]
    third = cell_edge[:, 2 : columns + 3]
    fourth = cell_edge[:, 3 : columns + 4]
    faces = wind_faces * limited(first, second, third, fourth)
    position = tile_start + lax.broadcasted_iota(jnp.int32, faces.shape, 1)
    flux_x = jnp.where(position == 0, 0.0, faces)
    return (flux_x, face_fluxes(cells, winds[1], 2), face_fluxes(cells, winds[2], 0))


def shards(species_slot, bulk, winds, fractions):
    slots_held = bulk.shape[0]
    columns = bulk.shape[2]
    tile_start = lax.axis_index("tile") * columns
    above = shifted(winds[0][:, 0:1, :], "tile", -1)
    wind_faces = jnp.concatenate([winds[0], above], axis=1)
    share_edge = extended(fractions, (("tile", 3),), 1)
    results = []
    for species_index in range(fractions.shape[0]):
        slot_number = species_slot[species_index]
        holder = slot_number // slots_held
        cells_here = lax.dynamic_index_in_dim(bulk, slot_number % slots_held, 0, keepdims=False)
        cells = broadcast(cells_here, "tag", holder)
        flux_x, flux_y, flux_z = all_fluxes(cells, rimmed(cells), wind_faces, winds, tile_start)
        edges = share_edge[species_index]
        shares = fractions[species_index]
        lower = edges[:, :, 0 : columns + 1]
        higher = edges[:, :, 1 : columns + 2]
        carried = jnp.maximum(flux_x, 0.0) * lower + jnp.minimum(flux_x, 0.0) * higher
        total = carried[:, :, 1:] - carried[:, :, :-1] + tag_divergence(shares, flux_y, 3)
        total = total + tag_divergence(shares, flux_z, 1)
        results.append((shares * cells - total).astype(jnp.bfloat16))
    return jnp.stack(results)


def solution(mesh):
    placed = (
        P(),
        P("tag", None, "tile", None),
        P(None, None, "tile", None),
        P(None, "tag", None, "tile", None),
    )
    return jax.shard_map(
        shards,
        mesh=mesh,
        in_specs=placed,
        out_specs=P(None, "tag", None, "tile", None),
        check_vma=False,
    )
```

profile of v0, /device:TPU:0, one launch (start us, length us, event | category | flops | bytes accessed | tf_op | source)
XLA Modules:
  0.0 128.6 jit_solution(11717660370264873853)
XLA Ops:
  6.5 0.0 all-reduce.15.cloned.1.call-start
  6.5 0.9 slice_bitcast_fusion.4
  7.5 1.3 %collective-permute-start = (f32[8,1,128]{2,1,0:T(1,128)S(1)}, f32[8,1,128]{2,1,0:T(1,128)S(1)}, u32[]{:S(2)}, u32[]{:S(2)}) collective-permute-start(f32[8,1,128]{2,1,0:T(1,128)S(1)} %slice.215), channel_id=1, source_target_pairs={{1,0},{2,1},{3,2},{5,4},{6,5},{7,6},{9,8},{10,9},{11,10},{13,12},{... | collective-permute-start | bytes 12296 | tf_op jit(solution)/shard_map/ppermute | solution.py:23
  8.8 1.4 %fusion.60 = (bf16[2,16,8,1,128]{4,3,2,1,0:T(2,128)(2,1)S(1)}, bf16[2,16,8,1,128]{4,3,2,1,0:T(2,128)(2,1)S(1)}) fusion(bf16[2,16,8,32,128]{4,3,2,1,0:T(8,128)(2,1)} %param.7), kind=kLoop, calls=%fused_computation.109 | loop fusion | bytes 262144 | tf_op jit(solution)/shard_map/slice | solution.py:13
  10.2 3.0 %collective-permute-start.3 = (bf16[2,16,8,1,128]{4,3,2,1,0:T(2,128)(2,1)S(1)}, bf16[2,16,8,1,128]{4,3,2,1,0:T(2,128)(2,1)S(1)}, u32[]{:S(2)}, u32[]{:S(2)}) collective-permute-start(bf16[2,16,8,1,128]{4,3,2,1,0:T(2,128)(2,1)S(1)} %get-tuple-element.23), channel_id=1, source_target_pairs={{0,1},{1,2},{2,3},{4,5},{5,6},{6,7},{8,9},{9,10},{10,11},{12,13},{... | collective-permute-start | bytes 196616 | tf_op jit(solution)/shard_map/ppermute | solution.py:12
  13.2 1.3 %collective-permute-start.4 = (bf16[2,16,8,1,128]{4,3,2,1,0:T(2,128)(2,1)S(1)}, bf16[2,16,8,1,128]{4,3,2,1,0:T(2,128)(2,1)S(1)}, u32[]{:S(2)}, u32[]{:S(2)}) collective-permute-start(bf16[2,16,8,1,128]{4,3,2,1,0:T(2,128)(2,1)S(1)} %get-tuple-element.24), channel_id=1, source_target_pairs={{1,0},{2,1},{3,2},{5,4},{6,5},{7,6},{9,8},{10,9},{11,10},{13,12},{... | collective-permute-start | bytes 196616 | tf_op jit(solution)/shard_map/ppermute | solution.py:15
  14.5 1.3 %fusion.63 = (s32[1]{0:T(128)}, s32[1]{0:T(128)}) fusion(s32[16]{0:T(128)} %param.4), kind=kLoop, calls=%fused_computation.112 | loop fusion | bytes 16 | tf_op jit(solution)/shard_map/slice | solution.py:84
  20.8 1.7 %select_bitcast_fusion.1 = (f32[8,32,128]{2,1,0:T(8,128)}, f32[8,32,128]{2,1,0:T(8,128)}) fusion(f32[2,8,32,128]{3,2,1,0:T(8,128)} %param.5, s32[]{:T(128)S(6)} %select_n.68, pred[]{:T(512)S(6)} %eq.28, s32[]{:T(128)S(6)} %select_n.77, pred[]{:T(512)S(6)} %eq.32), kind=kLoop, calls=%fused_computation.91 | loop fusion | flops 65536 | bytes 524298 | tf_op jit(solution)/shard_map/jit(_where)/select_n | solution.py:27
  22.5 0.0 all-reduce.15.cloned.1.call-update
  22.5 0.6 iota_compare_fusion
  23.1 0.0 copy-start
  23.1 3.6 %slice_bitcast_fusion.3 = (bf16[16,8,32,128]{3,2,1,0:T(8,128)(2,1)}, bf16[16,8,32,128]{3,2,1,0:T(8,128)(2,1)}) fusion(bf16[2,16,8,32,128]{4,3,2,1,0:T(8,128)(2,1)} %param.7), kind=kLoop, calls=%fused_computation.31 | loop fusion | bytes 4194304 | tf_op jit(solution)/shard_map/squeeze | solution.py:90
  26.7 0.0 collective-permute-done.3
  26.7 0.0 collective-permute-done.4
  26.8 0.0 copy-done
  26.8 1.5 %pad_maximum_fusion = bf16[2,16,8,34,128]{4,3,2,1,0:T(8,128)(2,1)S(1)} fusion(bf16[2,16,8,1,128]{4,3,2,1,0:T(2,128)(2,1)S(1)} %collective-permute-done.4, bf16[2,16,8,32,128]{4,3,2,1,0:T(8,128)(2,1)S(1)} %copy-done, bf16[2,16,8,1,128]{4,3,2,1,0:T(2,128)(2,1)S(1)} %collective-permute-done.3), kind=kLoop, calls=%fused_computation.6 | loop fusion | flops 6684672 | bytes 4456448 | tf_op jit(solution)/shard_map/concatenate | solution.py:16
  28.3 1.5 %slice_bitcast_fusion.1 = (bf16[16,8,34,128]{3,2,1,0:T(8,128)(2,1)S(1)}, bf16[16,8,34,128]{3,2,1,0:T(8,128)(2,1)}) fusion(bf16[2,16,8,34,128]{4,3,2,1,0:T(8,128)(2,1)S(1)} %pad_maximum_fusion), kind=kLoop, calls=%fused_computation.27 | loop fusion | bytes 4456448 | tf_op jit(solution)/shard_map/squeeze | solution.py:89
  29.8 68.8 %all-reduce.15.cloned.1.call-done = (f32[8,32,128]{2,1,0:T(8,128)}, f32[8,32,128]{2,1,0:T(8,128)}) async-done(((f32[8,32,128]{2,1,0:T(8,128)}, f32[8,32,128]{2,1,0:T(8,128)}), (f32[8,32,128]{2,1,0:T(8,128)}, f32[8,32,128]{2,1,0:T(8,128)})) %all-reduce.15.cloned.1.call-update) | async-done | bytes 262160 | tf_op jit(solution)/shard_map/psum | solution.py:28
  98.6 0.0 copy-start.2
  98.6 0.0 copy-start.3
  98.6 2.5 %broadcast_maximum_fusion.3 = (f32[8,32,128]{2,1,0:T(8,128)S(1)}, f32[8,32,128]{2,1,0:T(8,128)S(1)}, f32[8,32,128]{2,1,0:T(8,128)S(1)}, f32[8,32,128]{2,1,0:T(8,...) fusion(f32[8,32,128]{2,1,0:T(8,128)} %get-tuple-element.5, ...), kind=kLoop, calls=%fused_computation.101 | loop fusion | flops 1638400 | bytes 1704072 | tf_op jit(solution)/shard_map/max | solution.py:54
  101.2 1.3 %collective-permute-start.5 = (bf16[8,2,128]{2,1,0:T(2,128)(2,1)S(1)}, bf16[8,2,128]{2,1,0:T(2,128)(2,1)S(1)}, u32[]{:S(2)}, u32[]{:S(2)}) collective-permute-start(bf16[8,2,128]{2,1,0:T(2,128)(2,1)S(1)} %get-tuple-element.45), channel_id=1, source_target_pairs={{0,1},{1,2},{2,3},{4,5},{5,6},{6,7},{8,9},{9,10},{10,11},{12,13},{... | collective-permute-start | bytes 12296 | tf_op jit(solution)/shard_map/ppermute | solution.py:12
  102.5 1.3 %collective-permute-start.6 = (bf16[8,2,128]{2,1,0:T(2,128)(2,1)S(1)}, bf16[8,2,128]{2,1,0:T(2,128)(2,1)S(1)}, u32[]{:S(2)}, u32[]{:S(2)}) collective-permute-start(bf16[8,2,128]{2,1,0:T(2,128)(2,1)S(1)} %get-tuple-element.46), channel_id=1, source_target_pairs={{1,0},{2,1},{3,2},{5,4},{6,5},{7,6},{9,8},{10,9},{11,10},{13,12},{... | collective-permute-start | bytes 12296 | tf_op jit(solution)/shard_map/ppermute | solution.py:15
  103.8 4.7 %collective-permute-start.1 = (bf16[8,2,128]{2,1,0:T(2,128)(2,1)S(1)}, bf16[8,2,128]{2,1,0:T(2,128)(2,1)S(1)}, u32[]{:S(2)}, u32[]{:S(2)}) collective-permute-start(bf16[8,2,128]{2,1,0:T(2,128)(2,1)S(1)} %get-tuple-element.43), channel_id=1, source_target_pairs={{0,1},{1,2},{2,3},{4,5},{5,6},{6,7},{8,9},{9,10},{10,11},{12,13},{... | collective-permute-start | bytes 12296 | tf_op jit(solution)/shard_map/ppermute | solution.py:12
  108.5 1.3 %collective-permute-start.2 = (bf16[8,2,128]{2,1,0:T(2,128)(2,1)S(1)}, bf16[8,2,128]{2,1,0:T(2,128)(2,1)S(1)}, u32[]{:S(2)}, u32[]{:S(2)}) collective-permute-start(bf16[8,2,128]{2,1,0:T(2,128)(2,1)S(1)} %get-tuple-element.44), channel_id=1, source_target_pairs={{1,0},{2,1},{3,2},{5,4},{6,5},{7,6},{9,8},{10,9},{11,10},{13,12},{... | collective-permute-start | bytes 12296 | tf_op jit(solution)/shard_map/ppermute | solution.py:15
  109.9 0.0 copy-done.2
  109.9 0.0 copy-done.3
  109.9 1.8 %fusion.2 = (f32[16,8,32,128]{3,2,1,0:T(8,128)S(1)}, f32[16,8,32,128]{3,2,1,0:T(8,128)S(1)}, f32[16,8,32,128]{3,2,1,0:T(8,128)S(1)}, f32[16,8,32,128]{3,2,1,0:T(8,128)S(1)}) fusion(bf16[16,8,32,128]{3,2,1,0:T(8,128)(2,1)S(1)} %copy-done.3, f32[8,32,128]{2,1,0:T(8,128)S(1)} %broadcast_minimum_fusion.5, f32[8,32,128]{2,1,0:T(8,128)S(1)} %get-tuple-element.35, ...), kind=kLoop, calls=%fused_computation.11 | loop fusion | flops 9437184 | bytes 11534336 | tf_op jit(solution)/shard_map/add | solution.py:54
  111.7 0.6 slice.227
  112.3 0.1 slice.228
  112.4 0.1 slice.241
  112.6 0.6 slice.240
  113.2 0.0 copy-start.1
  113.2 0.0 collective-permute-done.1
  113.2 0.0 collective-permute-done.2
  113.3 0.0 collective-permute-done.5
  113.3 0.0 collective-permute-done.6
  113.3 0.0 collective-permute-done
  113.3 0.2 broadcast_maximum_fusion.1
  113.6 0.9 copy-done.1
  114.5 0.0 copy-start.5
  114.5 2.2 %multiply_add_fusion = (f32[16,8,33,128]{3,2,1,0:T(8,128)S(1)}, f32[16,8,33,128]{3,2,1,0:T(8,128)S(1)}) fusion(bf16[16,8,34,128]{3,2,1,0:T(8,128)(2,1)S(1)} %copy-done.1, f32[8,33,128]{2,1,0:T(8,128)S(1)} %broadcast_minimum_fusion, f32[8,33,128]{2,1,0:T(8,128)S(1)} %get-tuple-element.39, bf16[16,8,34,128]{3,2,1,0:T(8,128)(2,1)S(1)} %get-tuple-element.19, ...), kind=kLoop, calls=%fused_computation.7 | loop fusion | flops 5406720 | bytes 9191424 | tf_op jit(solution)/shard_map/add | solution.py:93
  116.8 0.0 copy-done.5
  116.8 0.0 copy-start.4
  116.8 1.7 %fusion.13 = bf16[1,16,8,32,128]{4,3,2,1,0:T(8,128)(2,1)S(1)} fusion(f32[16,7,32,128]{3,2,1,0:T(8,128)S(1)} %slice.228, f32[16,8,32,127]{3,2,1,0:T(8,128)S(1)} %slice.227, f32[16,8,33,128]{3,2,1,0:T(8,128)S(1)} %get-tuple-element.52, f32[8,32,128]{2,1,0:T(8,128)S(1)} %copy-done.5, bf16[2,16,8,32,128]{4,3,2,1,0:T(8,128)(2,1)S(1)} %copy-done, ...), kind=kLoop, calls=%fused_computation.33 | loop fusion | flops 9437184 | bytes 11911168 | tf_op jit(solution)/shard_map/stack | solution.py:97
  118.5 0.0 copy-done.4
  118.5 1.7 %fusion.12 = bf16[1,16,8,32,128]{4,3,2,1,0:T(8,128)(2,1)S(1)} fusion(f32[16,7,32,128]{3,2,1,0:T(8,128)S(1)} %slice.241, f32[16,8,32,127]{3,2,1,0:T(8,128)S(1)} %slice.240, f32[16,8,33,128]{3,2,1,0:T(8,128)S(1)} %get-tuple-element.51, f32[8,32,128]{2,1,0:T(8,128)S(1)} %copy-done.4, bf16[2,16,8,32,128]{4,3,2,1,0:T(8,128)(2,1)S(1)} %copy-done, ...), kind=kLoop, calls=%fused_computation.32 | loop fusion | flops 9437184 | bytes 11911168 | tf_op jit(solution)/shard_map/stack | solution.py:97
  120.3 1.5 %pad_maximum_fusion.1 = bf16[2,16,8,32,128]{4,3,2,1,0:T(8,128)(2,1)} fusion(bf16[1,16,8,32,128]{4,3,2,1,0:T(8,128)(2,1)S(1)} %fusion.12, bf16[1,16,8,32,128]{4,3,2,1,0:T(8,128)(2,1)S(1)} %fusion.13), kind=kLoop, calls=%fused_computation.23 | loop fusion | flops 1048576 | bytes 4194304 | tf_op jit(solution)/shard_map/stack | solution.py:97
  (13 shorter events, 0.2 us)
Async XLA Ops:
  6.5 92.1 %all-reduce.15.cloned.1.call-start = ((), (), s32[]{:S(2)}) async-start(), calls=%async_computation | async-start | bytes 524288 | tf_op jit(solution)/shard_map/psum | solution.py:28
  7.5 105.9 %collective-permute-start = (f32[8,1,128]{2,1,0:T(1,128)S(1)}, f32[8,1,128]{2,1,0:T(1,128)S(1)}, u32[]{:S(2)}, u32[]{:S(2)}) collective-permute-start(f32[8,1,128]{2,1,0:T(1,128)S(1)} %slice.215), channel_id=1, source_target_pairs={{1,0},{2,1},{3,2},{5,4},{6,5},{7,6},{9,8},{10,9},{11,10},{13,12},{... | collective-permute-start | bytes 12296 | tf_op jit(solution)/shard_map/ppermute | solution.py:23
  10.2 16.5 %collective-permute-start.3 = (bf16[2,16,8,1,128]{4,3,2,1,0:T(2,128)(2,1)S(1)}, bf16[2,16,8,1,128]{4,3,2,1,0:T(2,128)(2,1)S(1)}, u32[]{:S(2)}, u32[]{:S(2)}) collective-permute-start(bf16[2,16,8,1,128]{4,3,2,1,0:T(2,128)(2,1)S(1)} %get-tuple-element.23), channel_id=1, source_target_pairs={{0,1},{1,2},{2,3},{4,5},{5,6},{6,7},{8,9},{9,10},{10,11},{12,13},{... | collective-permute-start | bytes 196616 | tf_op jit(solution)/shard_map/ppermute | solution.py:12
  13.2 13.5 %collective-permute-start.4 = (bf16[2,16,8,1,128]{4,3,2,1,0:T(2,128)(2,1)S(1)}, bf16[2,16,8,1,128]{4,3,2,1,0:T(2,128)(2,1)S(1)}, u32[]{:S(2)}, u32[]{:S(2)}) collective-permute-start(bf16[2,16,8,1,128]{4,3,2,1,0:T(2,128)(2,1)S(1)} %get-tuple-element.24), channel_id=1, source_target_pairs={{1,0},{2,1},{3,2},{5,4},{6,5},{7,6},{9,8},{10,9},{11,10},{13,12},{... | collective-permute-start | bytes 196616 | tf_op jit(solution)/shard_map/ppermute | solution.py:15
  23.1 3.6 %copy-start = (bf16[2,16,8,32,128]{4,3,2,1,0:T(8,128)(2,1)S(1)}, bf16[2,16,8,32,128]{4,3,2,1,0:T(8,128)(2,1)}, u32[]{:S(2)}) copy-start(bf16[2,16,8,32,128]{4,3,2,1,0:T(8,128)(2,1)} %param.7) | copy-start | bytes 6291460
  98.6 11.3 %copy-start.2 = (bf16[16,8,32,128]{3,2,1,0:T(8,128)(2,1)S(1)}, bf16[16,8,32,128]{3,2,1,0:T(8,128)(2,1)}, u32[]{:S(2)}) copy-start(bf16[16,8,32,128]{3,2,1,0:T(8,128)(2,1)} %get-tuple-element.22) | copy-start | bytes 3145732
  98.6 11.3 %copy-start.3 = (bf16[16,8,32,128]{3,2,1,0:T(8,128)(2,1)S(1)}, bf16[16,8,32,128]{3,2,1,0:T(8,128)(2,1)}, u32[]{:S(2)}) copy-start(bf16[16,8,32,128]{3,2,1,0:T(8,128)(2,1)} %get-tuple-element.21) | copy-start | bytes 3145732
  101.2 12.1 %collective-permute-start.5 = (bf16[8,2,128]{2,1,0:T(2,128)(2,1)S(1)}, bf16[8,2,128]{2,1,0:T(2,128)(2,1)S(1)}, u32[]{:S(2)}, u32[]{:S(2)}) collective-permute-start(bf16[8,2,128]{2,1,0:T(2,128)(2,1)S(1)} %get-tuple-element.45), channel_id=1, source_target_pairs={{0,1},{1,2},{2,3},{4,5},{5,6},{6,7},{8,9},{9,10},{10,11},{12,13},{... | collective-permute-start | bytes 12296 | tf_op jit(solution)/shard_map/ppermute | solution.py:12
  102.5 10.8 %collective-permute-start.6 = (bf16[8,2,128]{2,1,0:T(2,128)(2,1)S(1)}, bf16[8,2,128]{2,1,0:T(2,128)(2,1)S(1)}, u32[]{:S(2)}, u32[]{:S(2)}) collective-permute-start(bf16[8,2,128]{2,1,0:T(2,128)(2,1)S(1)} %get-tuple-element.46), channel_id=1, source_target_pairs={{1,0},{2,1},{3,2},{5,4},{6,5},{7,6},{9,8},{10,9},{11,10},{13,12},{... | collective-permute-start | bytes 12296 | tf_op jit(solution)/shard_map/ppermute | solution.py:15
  103.8 9.4 %collective-permute-start.1 = (bf16[8,2,128]{2,1,0:T(2,128)(2,1)S(1)}, bf16[8,2,128]{2,1,0:T(2,128)(2,1)S(1)}, u32[]{:S(2)}, u32[]{:S(2)}) collective-permute-start(bf16[8,2,128]{2,1,0:T(2,128)(2,1)S(1)} %get-tuple-element.43), channel_id=1, source_target_pairs={{0,1},{1,2},{2,3},{4,5},{5,6},{6,7},{8,9},{9,10},{10,11},{12,13},{... | collective-permute-start | bytes 12296 | tf_op jit(solution)/shard_map/ppermute | solution.py:12
  108.5 4.7 %collective-permute-start.2 = (bf16[8,2,128]{2,1,0:T(2,128)(2,1)S(1)}, bf16[8,2,128]{2,1,0:T(2,128)(2,1)S(1)}, u32[]{:S(2)}, u32[]{:S(2)}) collective-permute-start(bf16[8,2,128]{2,1,0:T(2,128)(2,1)S(1)} %get-tuple-element.44), channel_id=1, source_target_pairs={{1,0},{2,1},{3,2},{5,4},{6,5},{7,6},{9,8},{10,9},{11,10},{13,12},{... | collective-permute-start | bytes 12296 | tf_op jit(solution)/shard_map/ppermute | solution.py:15
  113.2 1.3 %copy-start.1 = (bf16[16,8,34,128]{3,2,1,0:T(8,128)(2,1)S(1)}, bf16[16,8,34,128]{3,2,1,0:T(8,128)(2,1)}, u32[]{:S(2)}) copy-start(bf16[16,8,34,128]{3,2,1,0:T(8,128)(2,1)} %get-tuple-element.20) | copy-start | bytes 3342340
  114.5 2.2 %copy-start.5 = (f32[8,32,128]{2,1,0:T(8,128)S(1)}, f32[8,32,128]{2,1,0:T(8,128)}, u32[]{:S(2)}) copy-start(f32[8,32,128]{2,1,0:T(8,128)} %get-tuple-element.6) | copy-start | bytes 393220
  116.8 1.8 %copy-start.4 = (f32[8,32,128]{2,1,0:T(8,128)S(1)}, f32[8,32,128]{2,1,0:T(8,128)}, u32[]{:S(2)}) copy-start(f32[8,32,128]{2,1,0:T(8,128)} %get-tuple-element.5) | copy-start | bytes 393220
Sparse Core Ops, SparseCore 0:
  22.6 75.9 all-reduce.14
where the time goes:
time: 131 us; the launch traced here: 129 us
  waiting for transfers between devices  68.8 us (53%)
  between operations  18.6 us (14%)
  other arithmetic  15.7 us (12%)
  starting transfers between devices  14.2 us (11%)
  local copies, waits for them, and re-layouts  11.3 us (9%)
    psum x1, waiting for transfers between devices, broadcast(): return lax.psum(block, axis)  68.8 us
    ppermute x3, starting transfers between devices, extended(): lax.ppermute(lax.slice_in_dim(block, block.shape[dim] - width, None, axis...  9.07 us
    another operation x3, other arithmetic, shards(): return jnp.stack(results)  4.98 us
    ppermute x3, starting transfers between devices, extended(): lax.ppermute(lax.slice_in_dim(block, 0, width, axis=dim), axis, backward)  3.88 us
    squeeze x1, local copies, waits for them, and re-layouts, shards(): shares = fractions[species_index]  3.6 us
  transfers between devices with their start and end apart: 8, of which 1 were waited for; matrix products, arithmetic and copies ran while one was open for 14% of the time, Pallas kernels for 0%

commit v1 on v0

v1 whole, which is shorter than its diff:
```python
import functools

import jax
import jax.numpy as jnp
from jax import lax
from jax.experimental import pallas as pl
from jax.experimental.pallas import tpu as pltpu
from jax.sharding import PartitionSpec as P

F32 = jnp.float32
BF16 = jnp.bfloat16
PAD = 8


def paired(value, axis, flip):
    count = lax.axis_size(axis)
    return lax.ppermute(value, axis, [(i, flip(i, count)) for i in range(count)])


def inner(i, count):
    return i ^ 1


def outer(i, count):
    return (i + 1) % count if i % 2 else (i - 1) % count


def limited(before_two, before, after, after_two):
    centred = (7.0 * (before + after) - (before_two + after_two)) / 12.0
    return jnp.minimum(jnp.maximum(centred, jnp.minimum(before, after)), jnp.maximum(before, after))


def pick_kernel(slots_ref, bulk_ref, main_ref, inner_ref, outer_ref):
    held, levels, columns, _ = bulk_ref.shape
    group = lax.axis_index("tag")
    even = lax.axis_index("tile") % 2 == 0
    for k in range(2):
        slot = slots_ref[lax.rem(group + k, 2)]
        mine = slot // held == group
        at = lax.rem(slot, held)
        main_ref[k] = jnp.where(mine, bulk_ref[at], 0.0).astype(BF16)
        for j in range(2):
            low = jnp.where(mine, bulk_ref[at, :, j, :], 0.0)
            high = jnp.where(mine, bulk_ref[at, :, columns - 2 + j, :], 0.0)
            rows = slice((2 * k + j) * levels, (2 * k + j + 1) * levels)
            inner_ref[rows, :] = jnp.where(even, high, low).astype(BF16)
            outer_ref[rows, :] = jnp.where(even, low, high).astype(BF16)


def picked(slots, bulk):
    held, levels, columns, lanes = bulk.shape
    return pl.pallas_call(
        pick_kernel,
        out_shape=(
            jax.ShapeDtypeStruct((2, levels, columns, lanes), BF16),
            jax.ShapeDtypeStruct((4 * levels, lanes), BF16),
            jax.ShapeDtypeStruct((4 * levels, lanes), BF16),
        ),
        in_specs=[
            pl.BlockSpec(memory_space=pltpu.SMEM),
            pl.BlockSpec(memory_space=pltpu.VMEM),
        ],
        out_specs=[pl.BlockSpec(memory_space=pltpu.VMEM)] * 3,
        name="pick",
    )(slots, bulk)


def advect_kernel(
    species_ref, cells_ref, rim_ref, winds_ref, above_ref, low_ref, high_ref, f_ref, _, out_ref,
    cell_ext, wind_ext, flux_ext, coef, share_ext,
):
    levels, columns, lanes = cells_ref.shape
    body = pl.ds(PAD, columns)
    first_tile = lax.axis_index("tile") == 0

    @pl.when(pl.program_id(0) == 0)
    def _():
        cell_ext[:, body, :] = cells_ref[...].astype(F32)
        rim = rim_ref[...].astype(F32)
        for j, row in enumerate((PAD - 2, PAD - 1, PAD + columns, PAD + columns + 1)):
            cell_ext[:, row, :] = rim[j * levels : (j + 1) * levels]
        wind_ext[:, 0:columns, :] = winds_ref[0]
        wind_ext[:, 0, :] = jnp.where(first_tile, 0.0, winds_ref[0, :, 0, :])
        wind_ext[:, columns, :] = above_ref[...].astype(F32)
        lane = lax.broadcasted_iota(jnp.int32, (columns, lanes), 1)
        faces = pl.ds(0, columns + 8)
        plane = [cell_ext[z, body, :] for z in range(levels)]
        zero = jnp.zeros_like(plane[0])
        at = lambda z: plane[z] if 0 <= z < levels else zero
        flux_z = [zero]
        for z in range(1, levels):
            flux_z.append(winds_ref[2, z] * limited(at(z - 2), at(z - 1), at(z), at(z + 1)))
        flux_z.append(zero)
        for z in range(levels):
            flux_ext[z, faces, :] = wind_ext[z] * limited(
                *(cell_ext[z, pl.ds(PAD - 2 + k, columns + 8), :] for k in range(4))
            )
            x_low = flux_ext[z, pl.ds(0, columns), :]
            x_up = flux_ext[z, pl.ds(1, columns), :]
            c = plane[z]
            y_two = jnp.where(lane < 2, 0.0, pltpu.roll(c, 2, 1))
            y_one = jnp.where(lane < 1, 0.0, pltpu.roll(c, 1, 1))
            y_next = jnp.where(lane == lanes - 1, 0.0, pltpu.roll(c, lanes - 1, 1))
            y_low = winds_ref[1, z] * limited(y_two, y_one, c, y_next)
            y_low = jnp.where(lane < 1, 0.0, y_low)
            y_up = pltpu.roll(y_low, lanes - 1, 1)
            centre = c
            for d, (low, up) in enumerate(((x_low, x_up), (y_low, y_up), (flux_z[z], flux_z[z + 1]))):
                inward = jnp.minimum(low, 0.0)
                outward = jnp.maximum(up, 0.0)
                coef[2 * d, z] = low - inward
                coef[2 * d + 1, z] = outward - up
                centre = centre + (inward - outward)
            coef[6, z] = centre

    def one_tag(i, carry):
        share_ext[:, PAD - 1, :] = low_ref[i].astype(F32)
        share_ext[:, PAD + columns, :] = high_ref[i].astype(F32)
        plane = [f_ref[i, z].astype(F32) for z in range(levels)]
        for z in range(levels):
            share_ext[z, body, :] = plane[z]
        for z in range(levels):
            f = plane[z]
            total = coef[6, z] * f
            total += coef[0, z] * share_ext[z, pl.ds(PAD - 1, columns), :]
            total += coef[1, z] * share_ext[z, pl.ds(PAD + 1, columns), :]
            total += coef[2, z] * pltpu.roll(f, 1, 1)
            total += coef[3, z] * pltpu.roll(f, lanes - 1, 1)
            if z > 0:
                total += coef[4, z] * plane[z - 1]
            if z < levels - 1:
                total += coef[5, z] * plane[z + 1]
            out_ref[i, z] = total.astype(out_ref.dtype)
        return carry

    lax.fori_loop(0, f_ref.shape[0], one_tag, 0)


def advected(which, cells, rim, winds, above, low, high, fractions, out, step):
    species, tags, levels, columns, lanes = fractions.shape
    whole = pl.BlockSpec(memory_space=pltpu.VMEM)
    halo = pl.BlockSpec((None, step, levels, lanes), lambda i, s: (s[0], i, 0, 0))
    block = pl.BlockSpec((None, step, levels, columns, lanes), lambda i, s: (s[0], i, 0, 0, 0))
    alias = {8: 0} if out is not None else {}
    if out is None:
        out = jnp.zeros((8, 128), BF16)
    return pl.pallas_call(
        advect_kernel,
        out_shape=jax.ShapeDtypeStruct(fractions.shape, fractions.dtype),
        grid_spec=pltpu.PrefetchScalarGridSpec(
            num_scalar_prefetch=1,
            grid=(tags // step,),
            in_specs=[whole, whole, whole, whole, halo, halo, block, pl.BlockSpec(memory_space=pl.ANY)],
            out_specs=block,
            scratch_shapes=[
                pltpu.VMEM((levels, columns + 24, lanes), F32),
                pltpu.VMEM((levels, columns + 8, lanes), F32),
                pltpu.VMEM((levels, columns + 8, lanes), F32),
                pltpu.VMEM((7, levels, columns, lanes), F32),
                pltpu.VMEM((levels, columns + 16, lanes), F32),
            ],
        ),
        input_output_aliases=alias,
        name="advect",
    )(which, cells, rim, winds, above, low, high, fractions, out)


def shards(species_slot, bulk, winds, fractions):
    held, levels, columns, lanes = bulk.shape
    species, tags = fractions.shape[:2]
    group, tile = lax.axis_index("tag"), lax.axis_index("tile")
    groups, tiles = lax.axis_size("tag"), lax.axis_size("tile")
    even = tile % 2 == 0

    main, inner_edge, outer_edge = picked(species_slot, bulk)
    from_inner = paired(inner_edge, "tile", inner)
    from_outer = paired(outer_edge, "tile", outer)
    low = jnp.where(even, from_outer, from_inner).reshape(2, 2 * levels, lanes)
    high = jnp.where(even, from_inner, from_outer).reshape(2, 2 * levels, lanes)
    low = jnp.where(tile == 0, jnp.zeros_like(low), low)
    high = jnp.where(tile == tiles - 1, jnp.zeros_like(high), high)
    rows = jnp.concatenate([main.reshape(2, levels * columns, lanes), low, high], axis=1)

    own = rows[0] + paired(rows[1], "tag", inner)
    bit = 2
    while bit < groups:
        own = own + paired(own, "tag", lambda i, count: i ^ bit)
        bit *= 2
    other = paired(own, "tag", inner)

    first, last = fractions[:, :, :, 0, :], fractions[:, :, :, columns - 1, :]
    top = winds[0, :, 0, :].astype(BF16)
    size = species * tags * levels
    inner_rows = jnp.concatenate([jnp.where(even, last, first).reshape(size, lanes), top])
    outer_rows = jnp.concatenate([jnp.where(even, first, last).reshape(size, lanes), top])
    got_inner = paired(inner_rows, "tile", inner)
    got_outer = paired(outer_rows, "tile", outer)
    below = jnp.where(even, got_outer, got_inner)
    beyond = jnp.where(even, got_inner, got_outer)
    below = jnp.where(tile == 0, jnp.zeros_like(below), below)
    beyond = jnp.where(tile == tiles - 1, jnp.zeros_like(beyond), beyond)
    share_low = below[:size].reshape(species, tags, levels, lanes)
    share_high = beyond[:size].reshape(species, tags, levels, lanes)
    above = beyond[size:]

    step = 4
    out = None
    for k, cells in enumerate((own, other)):
        which = (lax.rem(group + k, 2))[None]
        out = advected(
            which, cells[: levels * columns].reshape(levels, columns, lanes), cells[levels * columns :],
            winds, above, share_low, share_high, fractions, out, step,
        )
    return out


def solution(mesh):
    placed = (
        P(),
        P("tag", None, "tile", None),
        P(None, None, "tile", None),
        P(None, "tag", None, "tile", None),
    )
    return jax.shard_map(
        shards,
        mesh=mesh,
        in_specs=placed,
        out_specs=P(None, "tag", None, "tile", None),
        check_vma=False,
    )
```

time: 131 us -> 38.2 us (0.29); the launches traced: 129 us -> 37.8 us
  waiting for transfers between devices: 68.8 us -> 5.12 us
  between operations: 18.6 us -> 0.1 us
  other arithmetic: 15.7 us -> 1.68 us
  Pallas kernels: 0 us -> 11.4 us
  local copies, waits for them, and re-layouts: 11.3 us -> 6.42 us
    psum x1 -> x0, waiting for transfers between devices: 68.8 us -> none  [broadcast(): return lax.psum(block, axis)]
    pallas_call x0 -> x3, Pallas kernels: none -> 11.4 us  [the longest x2 9.73 us: advected(): pl.pallas_call(advect_kernel, out_shape=jax.ShapeDtypeStruct(fractions.sh...]
    squeeze x3 -> x1, local copies, waits for them, and re-layouts: 6.02 us -> 0.01 us  [shards(): own = rows[0] + paired(rows[1], 'tag', inner)]
    ppermute x7 -> x8, waiting for transfers between devices: 0.02 us -> 5.12 us  [paired(): lax.ppermute(value, axis, [(i, flip(i, count)) for i in range(count)])]
    another operation x3 -> x0, other arithmetic: 4.98 us -> none  [shards(): return jnp.stack(results)]
    add x2 -> x3, other arithmetic: 4.01 us -> 0.05 us  [the longest x2 0.05 us: shards(): own = own + paired(own, 'tag', lambda i, count: i ^ bit)]
    max x2 -> x0, other arithmetic: 2.68 us -> none  [the longest x1 2.48 us: tag_divergence(): carried = jnp.maximum(faces, 0.0) * lower + jnp.minimum(faces, 0.0) * shares]
    slice x9 -> x8, local copies, waits for them, and re-layouts: 4.28 us -> 5.82 us  [the longest x1 1.42 us: shards(): first, last = (fractions[:, :, :, 0, :], fractions[:, :, :, columns - 1, :])]
  transfers between devices with their start and end apart: 8 -> 8, of which waited for: 1 -> 3; matrix products, arithmetic and copies ran while one was open for 14% -> 16% of each run, Pallas kernels for 0% -> 13%
where the time goes in v1:
time: 38.2 us; the launch traced here: 37.8 us
  starting transfers between devices  13 us (34%)
  Pallas kernels  11.4 us (30%)
  local copies, waits for them, and re-layouts  6.42 us (17%)
  waiting for transfers between devices  5.12 us (13%)
  other arithmetic  1.68 us (4%)
    ppermute x8, starting transfers between devices, paired(): lax.ppermute(value, axis, [(i, flip(i, count)) for i in range(count)])  13 us
    pallas_call x2, Pallas kernels, advected(): pl.pallas_call(advect_kernel, out_shape=jax.ShapeDtypeStruct(fractions.sh...  9.73 us
    ppermute x8, waiting for transfers between devices, paired(): lax.ppermute(value, axis, [(i, flip(i, count)) for i in range(count)])  5.12 us
    pallas_call x1, Pallas kernels, picked(): pl.pallas_call(pick_kernel, out_shape=(jax.ShapeDtypeStruct((2, levels, c...  1.7 us
    slice x1, local copies, waits for them, and re-layouts, shards(): first, last = (fractions[:, :, :, 0, :], fractions[:, :, :, columns - 1, :])  1.42 us
    slice x2, local copies, waits for them, and re-layouts, shards(): cells[:levels * columns].reshape(levels, columns, lanes)  1.23 us
    slice x2, local copies, waits for them, and re-layouts, shards(): cells[levels * columns:]  1.18 us
    concatenate x1, other arithmetic, shards(): jnp.concatenate([main.reshape(2, levels * columns, lanes), low, high], ax...  0.92 us
  transfers between devices with their start and end apart: 8, of which 3 were waited for; matrix products, arithmetic and copies ran while one was open for 16% of the time, Pallas kernels for 13%

profile of v1, /device:TPU:0, one launch (start us, length us, event | category | flops | bytes accessed | tf_op | source)
XLA Modules:
  0.0 37.8 jit_solution(8038190660612628817)
XLA Ops:
  0.0 1.7 %pick.1 = (bf16[2,8,32,128]{3,2,1,0:T(8,128)(2,1)}, bf16[32,128]{1,0:T(8,128)(2,1)}, bf16[32,128]{1,0:T(8,128)(2,1)}) custom-call(s32[16]{0:T(128)} %slots_ref.1, f32[2,8,32,128]{3,2,1,0:T(8,128)} %bulk_ref.1), custom_call_target="tpu_custom_call" | custom-call | tf_op jit(solution)/shard_map/pick/pallas_call | solution.py:52
  1.7 2.4 %collective-permute-start = (bf16[32,128]{1,0:T(8,128)(2,1)}, bf16[32,128]{1,0:T(8,128)(2,1)S(1)}, u32[]{:S(2)}, u32[]{:S(2)}) collective-permute-start(bf16[32,128]{1,0:T(8,128)(2,1)} %get-tuple-element.9), channel_id=1, source_target_pairs={{0,3},{1,2},{2,1},{3,0},{4,7},{5,6},{6,5},{7,4},{8,11},{9,10},{10,... | collective-permute-start | bytes 24584 | tf_op jit(solution)/shard_map/ppermute | solution.py:17
  4.1 0.7 %collective-permute-start.1 = (bf16[32,128]{1,0:T(8,128)(2,1)}, bf16[32,128]{1,0:T(8,128)(2,1)S(1)}, u32[]{:S(2)}, u32[]{:S(2)}) collective-permute-start(bf16[32,128]{1,0:T(8,128)(2,1)} %get-tuple-element.10), channel_id=1, source_target_pairs={{0,1},{1,0},{2,3},{3,2},{4,5},{5,4},{6,7},{7,6},{8,9},{9,8},{10,11... | collective-permute-start | bytes 24584 | tf_op jit(solution)/shard_map/ppermute | solution.py:17
  4.8 1.4 %fusion.3 = (bf16[2,16,8,1,128]{4,3,2,1,0:T(2,128)(2,1)S(1)}, bf16[2,16,8,1,128]{4,3,2,1,0:T(2,128)(2,1)S(1)}) fusion(bf16[2,16,8,32,128]{4,3,2,1,0:T(8,128)(2,1)} %f_ref.3), kind=kLoop, calls=%fused_computation.15 | loop fusion | bytes 262144 | tf_op jit(solution)/shard_map/slice | solution.py:191
  6.3 0.0 collective-permute-done
  6.3 0.0 collective-permute-done.1
  6.3 0.9 %pad_maximum_fusion = bf16[2,288,128]{2,1,0:T(8,128)(2,1)S(1)} fusion(bf16[2,16,128]{2,1,0:T(8,128)(2,1)S(1)} %bitcast.30, bf16[2,16,128]{2,1,0:T(8,128)(2,1)S(1)} %bitcast.29, bf16[2,256,128]{2,1,0:T(8,128)(2,1)} %bitcast.28), kind=kLoop, calls=%fused_computation | loop fusion | flops 442368 | bytes 294912 | tf_op jit(solution)/shard_map/concatenate | solution.py:182
  7.2 1.8 %collective-permute-start.2 = (bf16[288,128]{1,0:T(8,128)(2,1)S(1)}, bf16[288,128]{1,0:T(8,128)(2,1)S(1)}, u32[]{:S(2)}, u32[]{:S(2)}) collective-permute-start(bf16[288,128]{1,0:T(8,128)(2,1)S(1)} %slice_bitcast_fusion), channel_id=1, source_target_pairs={{0,4},{4,0},{8,12},{12,8},{16,20},{20,16},{24,28},{28,24},{1,5},{5... | collective-permute-start | bytes 221192 | tf_op jit(solution)/shard_map/ppermute | solution.py:17
  9.0 0.8 %slice.53 = bf16[1,8,1,128]{3,2,1,0:T(2,128)(2,1)S(1)} slice(f32[3,8,32,128]{3,2,1,0:T(8,128)} %winds_ref.3), slice={[0:1], [0:8], [0:1], [0:128]} | slice | bytes 4096 | tf_op jit(solution)/shard_map/slice | solution.py:192
  9.8 1.9 %collective-permute-done.2 = bf16[288,128]{1,0:T(8,128)(2,1)S(1)} collective-permute-done((bf16[288,128]{1,0:T(8,128)(2,1)S(1)}, bf16[288,128]{1,0:T(8,128)(2,1)S(1)}, u32[]{:S(2)}, u32[]{:S(2)}) %collective-permute-start.2) | collective-permute-done | bytes 73760 | tf_op jit(solution)/shard_map/ppermute | solution.py:17
  11.7 1.8 %collective-permute-start.3 = (bf16[288,128]{1,0:T(8,128)(2,1)S(1)}, bf16[288,128]{1,0:T(8,128)(2,1)S(1)}, u32[]{:S(2)}, u32[]{:S(2)}) collective-permute-start(bf16[288,128]{1,0:T(8,128)(2,1)S(1)} %fusion), channel_id=1, source_target_pairs={{0,8},{4,12},{8,0},{12,4},{16,24},{20,28},{24,16},{28,20},{1,9},{5... | collective-permute-start | bytes 221192 | tf_op jit(solution)/shard_map/ppermute | solution.py:17
  13.5 0.1 collective-permute-start.7
  13.6 1.7 %collective-permute-start.6 = (bf16[264,128]{1,0:T(8,128)(2,1)S(1)}, bf16[264,128]{1,0:T(8,128)(2,1)S(1)}, u32[]{:S(2)}, u32[]{:S(2)}) collective-permute-start(bf16[264,128]{1,0:T(8,128)(2,1)S(1)} %get-tuple-element.18), channel_id=1, source_target_pairs={{0,1},{1,0},{2,3},{3,2},{4,5},{5,4},{6,7},{7,6},{8,9},{9,8},{10,11... | collective-permute-start | bytes 202760 | tf_op jit(solution)/shard_map/ppermute | solution.py:17
  15.3 0.8 %collective-permute-done.3 = bf16[288,128]{1,0:T(8,128)(2,1)S(1)} collective-permute-done((bf16[288,128]{1,0:T(8,128)(2,1)S(1)}, bf16[288,128]{1,0:T(8,128)(2,1)S(1)}, u32[]{:S(2)}, u32[]{:S(2)}) %collective-permute-start.3) | collective-permute-done | bytes 73760 | tf_op jit(solution)/shard_map/ppermute | solution.py:17
  16.1 2.8 %collective-permute-start.4 = (bf16[288,128]{1,0:T(8,128)(2,1)S(1)}, bf16[288,128]{1,0:T(8,128)(2,1)S(1)}, u32[]{:S(2)}, u32[]{:S(2)}) collective-permute-start(bf16[288,128]{1,0:T(8,128)(2,1)S(1)} %add.19), channel_id=1, source_target_pairs={{0,16},{4,20},{8,24},{12,28},{16,0},{20,4},{24,8},{28,12},{1,17},{... | collective-permute-start | bytes 221192 | tf_op jit(solution)/shard_map/ppermute | solution.py:17
  19.0 0.0 collective-permute-done.7
  19.0 0.0 collective-permute-done.6
  19.0 2.4 %collective-permute-done.4 = bf16[288,128]{1,0:T(8,128)(2,1)S(1)} collective-permute-done((bf16[288,128]{1,0:T(8,128)(2,1)S(1)}, bf16[288,128]{1,0:T(8,128)(2,1)S(1)}, u32[]{:S(2)}, u32[]{:S(2)}) %collective-permute-start.4) | collective-permute-done | bytes 73760 | tf_op jit(solution)/shard_map/ppermute | solution.py:17
  21.5 1.8 %collective-permute-start.5 = (bf16[288,128]{1,0:T(8,128)(2,1)S(1)}, bf16[288,128]{1,0:T(8,128)(2,1)S(1)}, u32[]{:S(2)}, u32[]{:S(2)}) collective-permute-start(bf16[288,128]{1,0:T(8,128)(2,1)S(1)} %add.20), channel_id=1, source_target_pairs={{0,4},{4,0},{8,12},{12,8},{16,20},{20,16},{24,28},{28,24},{1,5},{5... | collective-permute-start | bytes 221192 | tf_op jit(solution)/shard_map/ppermute | solution.py:17
  23.2 0.6 %fusion.1 = bf16[256,128]{1,0:T(8,128)(2,1)} fusion(bf16[264,128]{1,0:T(8,128)(2,1)S(1)} %collective-permute-done.6, bf16[264,128]{1,0:T(8,128)(2,1)S(1)} %collective-permute-done.7, pred[]{:T(512)S(6)} %eq.13, pred[]{:T(512)S(6)} %eq.14), kind=kLoop, calls=%fused_computation.8 | loop fusion | flops 65536 | bytes 196610 | tf_op jit(solution)/shard_map/jit(_where)/select_n | solution.py:200
  23.8 0.6 %slice.54.above_ref = bf16[8,128]{1,0:T(8,128)(2,1)} slice(bf16[264,128]{1,0:T(8,128)(2,1)S(1)} %select_select_fusion), slice={[256:264], [0:128]} | slice | bytes 4096 | tf_op jit(solution)/shard_map/slice | solution.py:204
  24.4 0.6 %slice.57 = bf16[256,128]{1,0:T(8,128)(2,1)} slice(bf16[264,128]{1,0:T(8,128)(2,1)S(1)} %select_select_fusion), slice={[0:256], [0:128]} | slice | bytes 131072 | tf_op jit(solution)/shard_map/slice | solution.py:203
  25.1 0.6 %slice.59.rim_ref = bf16[32,128]{1,0:T(8,128)(2,1)} slice(bf16[288,128]{1,0:T(8,128)(2,1)S(1)} %add.20), slice={[256:288], [0:128]} | slice | bytes 16384 | tf_op jit(solution)/shard_map/slice | solution.py:211
  25.7 0.6 %slice.58 = bf16[256,128]{1,0:T(8,128)(2,1)} slice(bf16[288,128]{1,0:T(8,128)(2,1)S(1)} %add.20), slice={[0:256], [0:128]} | slice | bytes 131072 | tf_op jit(solution)/shard_map/slice | solution.py:211
  26.3 0.6 %broadcast_in_dim.11._ = bf16[8,128]{1,0:T(8,128)(2,1)} broadcast(bf16[]{:T(256)} %constant.31.clone.1), dimensions={} | broadcast | bytes 2050 | tf_op jit(solution)/shard_map/broadcast_in_dim | solution.py:146
  26.9 4.9 %advect.2._ = bf16[2,16,8,32,128]{4,3,2,1,0:T(8,128)(2,1)} custom-call(s32[1]{0:T(128)} %bitcast.12.species_ref, bf16[8,32,128]{2,1,0:T(8,128)(2,1)} %bitcast.25, bf16[32,128]{1,0:T(8,128)(2,1)} %slice.59.rim_ref, f32[3,8,32,128]{3,2,1,0:T(8,128)} %winds_ref.3, bf16[8,128]{1,0:T(8,128)(2,1)} %slice.54.above_ref, bf16[2,16,8,128]{3,2,1,0:T(8,128)(2,1)} %bitcast.20, ...), custom_call_target="tpu_custom_call" | custom-call | tf_op jit(solution)/shard_map/advect/pallas_call | solution.py:147
  31.7 0.0 collective-permute-done.5
  31.7 0.6 %slice.52.rim_ref = bf16[32,128]{1,0:T(8,128)(2,1)} slice(bf16[288,128]{1,0:T(8,128)(2,1)S(1)} %collective-permute-done.5), slice={[256:288], [0:128]} | slice | bytes 16384 | tf_op jit(solution)/shard_map/slice | solution.py:211
  32.3 0.6 %slice.51 = bf16[256,128]{1,0:T(8,128)(2,1)} slice(bf16[288,128]{1,0:T(8,128)(2,1)S(1)} %collective-permute-done.5), slice={[0:256], [0:128]} | slice | bytes 131072 | tf_op jit(solution)/shard_map/slice | solution.py:211
  32.9 4.9 %advect.3 = bf16[2,16,8,32,128]{4,3,2,1,0:T(8,128)(2,1)} custom-call(s32[1]{0:T(128)} %bitcast.species_ref, bf16[8,32,128]{2,1,0:T(8,128)(2,1)} %bitcast.24, bf16[32,128]{1,0:T(8,128)(2,1)} %slice.52.rim_ref, f32[3,8,32,128]{3,2,1,0:T(8,128)} %winds_ref.3, bf16[8,128]{1,0:T(8,128)(2,1)} %slice.54.above_ref, ...), custom_call_target="tpu_custom_call", output_to_operand_aliasing={{}: (8, {})} | custom-call | tf_op jit(solution)/shard_map/advect/pallas_call | solution.py:147
  (9 shorter events, 0.1 us)
Async XLA Ops:
  1.7 4.6 %collective-permute-start = (bf16[32,128]{1,0:T(8,128)(2,1)}, bf16[32,128]{1,0:T(8,128)(2,1)S(1)}, u32[]{:S(2)}, u32[]{:S(2)}) collective-permute-start(bf16[32,128]{1,0:T(8,128)(2,1)} %get-tuple-element.9), channel_id=1, source_target_pairs={{0,3},{1,2},{2,1},{3,0},{4,7},{5,6},{6,5},{7,4},{8,11},{9,10},{10,... | collective-permute-start | bytes 24584 | tf_op jit(solution)/shard_map/ppermute | solution.py:17
  4.1 2.1 %collective-permute-start.1 = (bf16[32,128]{1,0:T(8,128)(2,1)}, bf16[32,128]{1,0:T(8,128)(2,1)S(1)}, u32[]{:S(2)}, u32[]{:S(2)}) collective-permute-start(bf16[32,128]{1,0:T(8,128)(2,1)} %get-tuple-element.10), channel_id=1, source_target_pairs={{0,1},{1,0},{2,3},{3,2},{4,5},{5,4},{6,7},{7,6},{8,9},{9,8},{10,11... | collective-permute-start | bytes 24584 | tf_op jit(solution)/shard_map/ppermute | solution.py:17
  7.2 4.4 %collective-permute-start.2 = (bf16[288,128]{1,0:T(8,128)(2,1)S(1)}, bf16[288,128]{1,0:T(8,128)(2,1)S(1)}, u32[]{:S(2)}, u32[]{:S(2)}) collective-permute-start(bf16[288,128]{1,0:T(8,128)(2,1)S(1)} %slice_bitcast_fusion), channel_id=1, source_target_pairs={{0,4},{4,0},{8,12},{12,8},{16,20},{20,16},{24,28},{28,24},{1,5},{5... | collective-permute-start | bytes 221192 | tf_op jit(solution)/shard_map/ppermute | solution.py:17
  11.7 4.4 %collective-permute-start.3 = (bf16[288,128]{1,0:T(8,128)(2,1)S(1)}, bf16[288,128]{1,0:T(8,128)(2,1)S(1)}, u32[]{:S(2)}, u32[]{:S(2)}) collective-permute-start(bf16[288,128]{1,0:T(8,128)(2,1)S(1)} %fusion), channel_id=1, source_target_pairs={{0,8},{4,12},{8,0},{12,4},{16,24},{20,28},{24,16},{28,20},{1,9},{5... | collective-permute-start | bytes 221192 | tf_op jit(solution)/shard_map/ppermute | solution.py:17
  13.5 5.4 %collective-permute-start.7 = (bf16[264,128]{1,0:T(8,128)(2,1)S(1)}, bf16[264,128]{1,0:T(8,128)(2,1)S(1)}, u32[]{:S(2)}, u32[]{:S(2)}) collective-permute-start(bf16[264,128]{1,0:T(8,128)(2,1)S(1)} %get-tuple-element.17), channel_id=1, source_target_pairs={{0,3},{1,2},{2,1},{3,0},{4,7},{5,6},{6,5},{7,4},{8,11},{9,10},{10,... | collective-permute-start | bytes 202760 | tf_op jit(solution)/shard_map/ppermute | solution.py:17
  13.6 5.4 %collective-permute-start.6 = (bf16[264,128]{1,0:T(8,128)(2,1)S(1)}, bf16[264,128]{1,0:T(8,128)(2,1)S(1)}, u32[]{:S(2)}, u32[]{:S(2)}) collective-permute-start(bf16[264,128]{1,0:T(8,128)(2,1)S(1)} %get-tuple-element.18), channel_id=1, source_target_pairs={{0,1},{1,0},{2,3},{3,2},{4,5},{5,4},{6,7},{7,6},{8,9},{9,8},{10,11... | collective-permute-start | bytes 202760 | tf_op jit(solution)/shard_map/ppermute | solution.py:17
  16.1 5.3 %collective-permute-start.4 = (bf16[288,128]{1,0:T(8,128)(2,1)S(1)}, bf16[288,128]{1,0:T(8,128)(2,1)S(1)}, u32[]{:S(2)}, u32[]{:S(2)}) collective-permute-start(bf16[288,128]{1,0:T(8,128)(2,1)S(1)} %add.19), channel_id=1, source_target_pairs={{0,16},{4,20},{8,24},{12,28},{16,0},{20,4},{24,8},{28,12},{1,17},{... | collective-permute-start | bytes 221192 | tf_op jit(solution)/shard_map/ppermute | solution.py:17
  21.5 10.3 %collective-permute-start.5 = (bf16[288,128]{1,0:T(8,128)(2,1)S(1)}, bf16[288,128]{1,0:T(8,128)(2,1)S(1)}, u32[]{:S(2)}, u32[]{:S(2)}) collective-permute-start(bf16[288,128]{1,0:T(8,128)(2,1)S(1)} %add.20), channel_id=1, source_target_pairs={{0,4},{4,0},{8,12},{12,8},{16,20},{20,16},{24,28},{28,24},{1,5},{5... | collective-permute-start | bytes 221192 | tf_op jit(solution)/shard_map/ppermute | solution.py:17

commit v2 on v0

v2 whole, which is shorter than its diff:
```python
import jax
import jax.numpy as jnp
from jax import lax
from jax.experimental import pallas as pl
from jax.experimental.pallas import tpu as pltpu
from jax.sharding import PartitionSpec as P


F32 = jnp.float32
BF16 = jnp.bfloat16
I16 = jnp.int16
PAD = 8
SCALE = 10240.0
TOGETHER = 4
LIMIT = pltpu.CompilerParams(vmem_limit_bytes=16 * 2**20)


def in_vmem(value):
    return pltpu.with_memory_space_constraint(value, pltpu.VMEM)


def in_hbm(value):
    return pltpu.with_memory_space_constraint(value, pltpu.HBM)


def paired(value, axis, flip):
    count = lax.axis_size(axis)
    return lax.ppermute(value, axis, [(i, flip(i, count)) for i in range(count)])


def inner(i, count):
    return i ^ 1


def outer(i, count):
    return (i + 1) % count if i % 2 else (i - 1) % count


def limited(before_two, before, after, after_two):
    centred = (7.0 * (before + after) - (before_two + after_two)) / 12.0
    return jnp.minimum(jnp.maximum(centred, jnp.minimum(before, after)), jnp.maximum(before, after))


def coded(values):
    return (values * SCALE + 0.5).astype(jnp.int32).astype(I16)


def decoded(codes):
    return codes.astype(jnp.int32).astype(F32) * (1.0 / SCALE)


def pick_kernel(slots_hbm, bulk_hbm, main_ref, inner_ref, outer_ref, slots_ref, bulk_ref, sems):
    held, levels, columns, _ = bulk_ref.shape
    table = pltpu.make_async_copy(slots_hbm, slots_ref, sems.at[0])
    field = pltpu.make_async_copy(bulk_hbm, bulk_ref, sems.at[1])
    table.start()
    field.start()
    group = lax.axis_index("tag")
    even = lax.axis_index("tile") % 2 == 0
    table.wait()
    field.wait()
    for k in range(2):
        slot = slots_ref[lax.rem(group + k, 2)]
        mine = slot // held == group
        at = lax.rem(slot, held)
        scale = jnp.where(mine, 1.0, 0.0)
        for z in range(levels):
            main_ref[k, pl.ds(z * columns, columns), :] = coded(bulk_ref[at, z] * scale)
        for j in range(2):
            low = bulk_ref[at, :, j, :]
            high = bulk_ref[at, :, columns - 2 + j, :]
            rows = pl.ds((2 * k + j) * levels, levels)
            inner_ref[rows, :] = coded(jnp.where(even, high, low) * scale)
            outer_ref[rows, :] = coded(jnp.where(even, low, high) * scale)


def picked(slots, bulk):
    _, levels, columns, lanes = bulk.shape
    whole = pl.BlockSpec(memory_space=pltpu.VMEM)
    far = pl.BlockSpec(memory_space=pltpu.HBM)
    edge = jax.ShapeDtypeStruct((4 * levels, lanes), I16)
    return pl.pallas_call(
        pick_kernel,
        out_shape=(jax.ShapeDtypeStruct((2, levels * columns, lanes), I16), edge, edge),
        in_specs=[far, far],
        out_specs=[whole] * 3,
        scratch_shapes=[
            pltpu.SMEM(slots.shape, slots.dtype),
            pltpu.VMEM(bulk.shape, bulk.dtype),
            pltpu.SemaphoreType.DMA((2,)),
        ],
        compiler_params=LIMIT,
        name="pick",
    )(in_hbm(slots), in_hbm(bulk))


def stage_kernel(f_hbm, winds_hbm, f_ref, winds_ref, inner_ref, outer_ref, sems):
    species, tags, levels, columns, _ = f_ref.shape
    even = lax.axis_index("tile") % 2 == 0
    parts = [(k, j) for k in range(species) for j in range(tags // TOGETHER)]
    copies = [pltpu.make_async_copy(winds_hbm, winds_ref, sems.at[len(parts)])]
    for n, (k, j) in enumerate(parts):
        part = pl.ds(j * TOGETHER, TOGETHER)
        copies.append(pltpu.make_async_copy(f_hbm.at[k, part], f_ref.at[k, part], sems.at[n]))
    for copy in copies:
        copy.start()
    copies[0].wait()
    rows = pl.ds(species * tags * levels, levels)
    top = winds_ref[0, :, 0, :].astype(BF16)
    inner_ref[rows, :] = top
    outer_ref[rows, :] = top
    for n, (k, j) in enumerate(parts):
        copies[n + 1].wait()
        for t in range(j * TOGETHER, (j + 1) * TOGETHER):
            first = f_ref[k, t, :, 0, :].astype(F32)
            last = f_ref[k, t, :, columns - 1, :].astype(F32)
            rows = pl.ds((k * tags + t) * levels, levels)
            inner_ref[rows, :] = jnp.where(even, last, first).astype(BF16)
            outer_ref[rows, :] = jnp.where(even, first, last).astype(BF16)


def staged(fractions, winds):
    species, tags, levels, _, lanes = fractions.shape
    whole = pl.BlockSpec(memory_space=pltpu.VMEM)
    far = pl.BlockSpec(memory_space=pltpu.HBM)
    rows = jax.ShapeDtypeStruct(((species * tags + 1) * levels, lanes), BF16)
    return pl.pallas_call(
        stage_kernel,
        out_shape=(
            jax.ShapeDtypeStruct(fractions.shape, fractions.dtype),
            jax.ShapeDtypeStruct(winds.shape, winds.dtype),
            rows,
            rows,
        ),
        in_specs=[far, far],
        out_specs=[whole] * 4,
        scratch_shapes=[pltpu.SemaphoreType.DMA((species * (tags // TOGETHER) + 1,))],
        compiler_params=LIMIT,
        name="stage",
    )(in_hbm(fractions), in_hbm(winds))


def advect_kernel(
    species_ref, cells_ref, winds_ref, inner_ref, outer_ref, f_ref, _, out_ref,
    cell_ext, wind_ext, flux_ext, coef, share_ext, result, sems,
):
    species, tags, levels, columns, lanes = f_ref.shape
    own = species_ref[0]
    body = pl.ds(PAD, columns)
    tile = lax.axis_index("tile")
    even = tile % 2 == 0
    last_tile = tile == lax.axis_size("tile") - 1

    def below(rows):
        return jnp.where(even, outer_ref[rows, :].astype(F32), inner_ref[rows, :].astype(F32))

    def beyond(rows):
        return jnp.where(even, inner_ref[rows, :].astype(F32), outer_ref[rows, :].astype(F32))

    for z in range(levels):
        cell_ext[z, body, :] = decoded(cells_ref[pl.ds(z * columns, columns), :])
    for j, row in enumerate((PAD - 2, PAD - 1, PAD + columns, PAD + columns + 1)):
        cell_ext[:, row, :] = decoded(cells_ref[pl.ds((columns + j) * levels, levels), :])
    wind_ext[:, 0:columns, :] = winds_ref[0]
    wind_ext[:, 0, :] = jnp.where(tile == 0, 0.0, winds_ref[0, :, 0, :])
    above = beyond(pl.ds(species * tags * levels, levels))
    wind_ext[:, columns, :] = jnp.where(last_tile, 0.0, above)
    lane = lax.broadcasted_iota(jnp.int32, (columns, lanes), 1)
    faces = pl.ds(0, columns + 8)
    plane = [cell_ext[z, body, :] for z in range(levels)]
    zero = jnp.zeros_like(plane[0])
    at = lambda z: plane[z] if 0 <= z < levels else zero
    flux_z = [zero]
    for z in range(1, levels):
        flux_z.append(winds_ref[2, z] * limited(at(z - 2), at(z - 1), at(z), at(z + 1)))
    flux_z.append(zero)
    for z in range(levels):
        flux_ext[z, faces, :] = wind_ext[z] * limited(
            *(cell_ext[z, pl.ds(PAD - 2 + k, columns + 8), :] for k in range(4))
        )
        x_low = flux_ext[z, pl.ds(0, columns), :]
        x_up = flux_ext[z, pl.ds(1, columns), :]
        c = plane[z]
        y_two = jnp.where(lane < 2, 0.0, pltpu.roll(c, 2, 1))
        y_one = jnp.where(lane < 1, 0.0, pltpu.roll(c, 1, 1))
        y_next = jnp.where(lane == lanes - 1, 0.0, pltpu.roll(c, lanes - 1, 1))
        y_low = winds_ref[1, z] * limited(y_two, y_one, c, y_next)
        y_low = jnp.where(lane < 1, 0.0, y_low)
        y_up = pltpu.roll(y_low, lanes - 1, 1)
        centre = c
        for d, (low, up) in enumerate(((x_low, x_up), (y_low, y_up), (flux_z[z], flux_z[z + 1]))):
            inward = jnp.minimum(low, 0.0)
            outward = jnp.maximum(up, 0.0)
            coef[2 * d, z] = low - inward
            coef[2 * d + 1, z] = outward - up
            centre = centre + (inward - outward)
        coef[6, z] = centre

    def some_tags(base, carry):
        planes = []
        for p in range(TOGETHER):
            i = base * TOGETHER + p
            rows = pl.ds((own * tags + i) * levels, levels)
            share_ext[p, :, PAD - 1, :] = below(rows)
            share_ext[p, :, PAD + columns, :] = beyond(rows)
            plane = [f_ref[own, i, z].astype(F32) for z in range(levels)]
            for z in range(levels):
                share_ext[p, z, body, :] = plane[z]
            planes.append(plane)
        for z in range(levels):
            cs = [coef[k, z] for k in range(7)]
            for p, plane in enumerate(planes):
                f = plane[z]
                total = cs[6] * f
                total += cs[0] * share_ext[p, z, pl.ds(PAD - 1, columns), :]
                total += cs[1] * share_ext[p, z, pl.ds(PAD + 1, columns), :]
                total += cs[2] * pltpu.roll(f, 1, 1)
                total += cs[3] * pltpu.roll(f, lanes - 1, 1)
                if z > 0:
                    total += cs[4] * plane[z - 1]
                if z < levels - 1:
                    total += cs[5] * plane[z + 1]
                result[base * TOGETHER + p, z] = total.astype(out_ref.dtype)
        return carry

    def stored(j):
        part = pl.ds(j * TOGETHER, TOGETHER)
        return pltpu.make_async_copy(result.at[part], out_ref.at[own, part], sems.at[j])

    for j in range(tags // TOGETHER):
        lax.fori_loop(j, j + 1, some_tags, 0)
        stored(j).start()
    for j in range(tags // TOGETHER):
        stored(j).wait()


def advected(which, cells, winds, from_inner, from_outer, fractions, out):
    _, tags, levels, columns, lanes = fractions.shape
    whole = pl.BlockSpec(memory_space=pltpu.VMEM)
    scalar = pl.BlockSpec(memory_space=pltpu.SMEM)
    place = pl.BlockSpec(memory_space=pl.ANY)
    first = out is None
    return pl.pallas_call(
        advect_kernel,
        out_shape=jax.ShapeDtypeStruct(fractions.shape, fractions.dtype),
        in_specs=[scalar, whole, whole, whole, whole, whole, scalar if first else place],
        out_specs=place,
        scratch_shapes=[
            pltpu.VMEM((levels, columns + 24, lanes), F32),
            pltpu.VMEM((levels, columns + 8, lanes), F32),
            pltpu.VMEM((levels, columns + 8, lanes), F32),
            pltpu.VMEM((7, levels, columns, lanes), F32),
            pltpu.VMEM((TOGETHER, levels, columns + 16, lanes), F32),
            pltpu.VMEM((tags, levels, columns, lanes), fractions.dtype),
            pltpu.SemaphoreType.DMA((tags // TOGETHER,)),
        ],
        input_output_aliases={} if first else {6: 0},
        compiler_params=LIMIT,
        name="advect",
    )(which, in_vmem(cells), winds, in_vmem(from_inner), in_vmem(from_outer), fractions, which if first else out)


def shards(species_slot, bulk, winds, fractions):
    _, levels, _, lanes = bulk.shape
    group, tile = lax.axis_index("tag"), lax.axis_index("tile")
    groups, tiles = lax.axis_size("tag"), lax.axis_size("tile")
    even = tile % 2 == 0

    main, inner_edge, outer_edge = picked(species_slot, bulk)
    from_outer = paired(outer_edge, "tile", outer)
    from_inner = paired(inner_edge, "tile", inner)
    low = jnp.where(even, from_outer, from_inner).reshape(2, 2 * levels, lanes)
    high = jnp.where(even, from_inner, from_outer).reshape(2, 2 * levels, lanes)
    low = jnp.where(tile == 0, jnp.zeros_like(low), low)
    high = jnp.where(tile == tiles - 1, jnp.zeros_like(high), high)
    rows = jnp.concatenate([main, low, high], axis=1)

    fractions, winds, inner_rows, outer_rows = staged(fractions, winds)
    got_inner = paired(inner_rows, "tile", inner)
    got_outer = paired(outer_rows, "tile", outer)

    crossed = paired(rows[1], "tag", inner)
    own = rows[0] + crossed
    bit = 2
    while bit < groups:
        came = paired(own, "tag", lambda i, count: i ^ bit)
        own = own + came
        bit *= 2
    other = paired(own, "tag", inner)

    out = None
    for k, cells in enumerate((own, other)):
        which = lax.rem(group + k, 2)[None]
        out = advected(which, cells, winds, got_inner, got_outer, fractions, out)
    return out


def solution(mesh):
    placed = (
        P(),
        P("tag", None, "tile", None),
        P(None, None, "tile", None),
        P(None, "tag", None, "tile", None),
    )
    return jax.shard_map(
        shards,
        mesh=mesh,
        in_specs=placed,
        out_specs=P(None, "tag", None, "tile", None),
        check_vma=False,
    )
```

time: 131 us -> 32.4 us (0.25); the launches traced: 129 us -> 32.3 us
  waiting for transfers between devices: 68.8 us -> 10.4 us
  between operations: 18.6 us -> 0.08 us
  other arithmetic: 15.7 us -> 0.09 us
  local copies, waits for them, and re-layouts: 11.3 us -> 0.01 us
  Pallas kernels: 0 us -> 7.8 us
    psum x1 -> x0, waiting for transfers between devices: 68.8 us -> none  [broadcast(): return lax.psum(block, axis)]
    ppermute x7 -> x8, waiting for transfers between devices: 0.02 us -> 10.4 us  [paired(): lax.ppermute(value, axis, [(i, flip(i, count)) for i in range(count)])]
    pallas_call x0 -> x4, Pallas kernels: none -> 7.8 us  [the longest x2 4.94 us: advected(): pl.pallas_call(advect_kernel, out_shape=jax.ShapeDtypeStruct(fractions.sh...]
    squeeze x3 -> x1, local copies, waits for them, and re-layouts: 6.02 us -> 0.01 us  [shards(): crossed = paired(rows[1], 'tag', inner)]
    another operation x3 -> x0, other arithmetic: 4.98 us -> none  [shards(): return jnp.stack(results)]
    slice x9 -> x0, local copies, waits for them, and re-layouts: 4.28 us -> none  [the longest x4 1.5 us: tag_divergence(): lax.slice_in_dim(carried, 1, length, axis=along)]
    add x2 -> x3, other arithmetic: 4.01 us -> 0.07 us  [the longest x2 0.05 us: shards(): own = own + came]
    max x2 -> x0, other arithmetic: 2.68 us -> none  [the longest x1 2.48 us: tag_divergence(): carried = jnp.maximum(faces, 0.0) * lower + jnp.minimum(faces, 0.0) * shares]
  transfers between devices with their start and end apart: 8 -> 8, of which waited for: 1 -> 6; matrix products, arithmetic and copies ran while one was open for 14% -> 0% of each run, Pallas kernels for 0% -> 13%
where the time goes in v2:
time: 32.4 us; the launch traced here: 32.3 us
  starting transfers between devices  13.9 us (43%)
  waiting for transfers between devices  10.4 us (32%)
  Pallas kernels  7.8 us (24%)
    ppermute x8, starting transfers between devices, paired(): lax.ppermute(value, axis, [(i, flip(i, count)) for i in range(count)])  13.9 us
    ppermute x8, waiting for transfers between devices, paired(): lax.ppermute(value, axis, [(i, flip(i, count)) for i in range(count)])  10.4 us
    pallas_call x2, Pallas kernels, advected(): pl.pallas_call(advect_kernel, out_shape=jax.ShapeDtypeStruct(fractions.sh...  4.94 us
    pallas_call x1, Pallas kernels, staged(): pl.pallas_call(stage_kernel, out_shape=(jax.ShapeDtypeStruct(fractions.sh...  1.76 us
    pallas_call x1, Pallas kernels, picked(): pl.pallas_call(pick_kernel, out_shape=(jax.ShapeDtypeStruct((2, levels *...  1.1 us
  transfers between devices with their start and end apart: 8, of which 6 were waited for; matrix products, arithmetic and copies ran while one was open for 0% of the time, Pallas kernels for 13%

profile of v2, /device:TPU:0, one launch (start us, length us, event | category | flops | bytes accessed | tf_op | source)
XLA Modules:
  0.0 32.3 jit_solution(6851451208851550923)
XLA Ops:
  0.0 1.1 %pick.1 = (s16[2,256,128]{2,1,0:T(8,128)(2,1)S(1)}, s16[32,128]{1,0:T(8,128)(2,1)S(1)}, s16[32,128]{1,0:T(8,128)(2,1)S(1)}) custom-call(s32[16]{0:T(128)} %slots_hbm.1, f32[2,8,32,128]{3,2,1,0:T(8,128)} %bulk_hbm.1), custom_call_target="tpu_custom_call" | custom-call | tf_op jit(solution)/shard_map/pick/pallas_call | solution.py:82
  1.1 2.5 %collective-permute-start = (s16[32,128]{1,0:T(8,128)(2,1)S(1)}, s16[32,128]{1,0:T(8,128)(2,1)S(1)}, u32[]{:S(2)}, u32[]{:S(2)}) collective-permute-start(s16[32,128]{1,0:T(8,128)(2,1)S(1)} %get-tuple-element.13), channel_id=1, source_target_pairs={{0,3},{1,2},{2,1},{3,0},{4,7},{5,6},{6,5},{7,4},{8,11},{9,10},{10,... | collective-permute-start | bytes 24584 | tf_op jit(solution)/shard_map/ppermute | solution.py:28
  3.6 0.7 %collective-permute-start.1 = (s16[32,128]{1,0:T(8,128)(2,1)S(1)}, s16[32,128]{1,0:T(8,128)(2,1)S(1)}, u32[]{:S(2)}, u32[]{:S(2)}) collective-permute-start(s16[32,128]{1,0:T(8,128)(2,1)S(1)} %get-tuple-element.14), channel_id=1, source_target_pairs={{0,1},{1,0},{2,3},{3,2},{4,5},{5,4},{6,7},{7,6},{8,9},{9,8},{10,11... | collective-permute-start | bytes 24584 | tf_op jit(solution)/shard_map/ppermute | solution.py:28
  4.3 0.7 %collective-permute-done = s16[32,128]{1,0:T(8,128)(2,1)S(1)} collective-permute-done((s16[32,128]{1,0:T(8,128)(2,1)S(1)}, s16[32,128]{1,0:T(8,128)(2,1)S(1)}, u32[]{:S(2)}, u32[]{:S(2)}) %collective-permute-start) | collective-permute-done | bytes 8224 | tf_op jit(solution)/shard_map/ppermute | solution.py:28
  5.0 0.1 collective-permute-done.1
  5.2 2.2 %collective-permute-start.2 = (s16[288,128]{1,0:T(8,128)(2,1)S(1)}, s16[288,128]{1,0:T(8,128)(2,1)S(1)}, u32[]{:S(2)}, u32[]{:S(2)}) collective-permute-start(s16[288,128]{1,0:T(8,128)(2,1)S(1)} %slice_bitcast_fusion), channel_id=1, source_target_pairs={{0,4},{4,0},{8,12},{12,8},{16,20},{20,16},{24,28},{28,24},{1,5},{5... | collective-permute-start | bytes 221192 | tf_op jit(solution)/shard_map/ppermute | solution.py:28
  7.3 2.6 %collective-permute-done.2 = s16[288,128]{1,0:T(8,128)(2,1)S(1)} collective-permute-done((s16[288,128]{1,0:T(8,128)(2,1)S(1)}, s16[288,128]{1,0:T(8,128)(2,1)S(1)}, u32[]{:S(2)}, u32[]{:S(2)}) %collective-permute-start.2) | collective-permute-done | bytes 73760 | tf_op jit(solution)/shard_map/ppermute | solution.py:28
  9.9 1.9 %collective-permute-start.3 = (s16[288,128]{1,0:T(8,128)(2,1)S(1)}, s16[288,128]{1,0:T(8,128)(2,1)S(1)}, u32[]{:S(2)}, u32[]{:S(2)}) collective-permute-start(s16[288,128]{1,0:T(8,128)(2,1)S(1)} %fusion), channel_id=1, source_target_pairs={{0,8},{4,12},{8,0},{12,4},{16,24},{20,28},{24,16},{28,20},{1,9},{5... | collective-permute-start | bytes 221192 | tf_op jit(solution)/shard_map/ppermute | solution.py:28
  11.9 2.5 %collective-permute-done.3 = s16[288,128]{1,0:T(8,128)(2,1)S(1)} collective-permute-done((s16[288,128]{1,0:T(8,128)(2,1)S(1)}, s16[288,128]{1,0:T(8,128)(2,1)S(1)}, u32[]{:S(2)}, u32[]{:S(2)}) %collective-permute-start.3) | collective-permute-done | bytes 73760 | tf_op jit(solution)/shard_map/ppermute | solution.py:28
  14.4 3.0 %collective-permute-start.4 = (s16[288,128]{1,0:T(8,128)(2,1)S(1)}, s16[288,128]{1,0:T(8,128)(2,1)S(1)}, u32[]{:S(2)}, u32[]{:S(2)}) collective-permute-start(s16[288,128]{1,0:T(8,128)(2,1)S(1)} %add.19), channel_id=1, source_target_pairs={{0,16},{4,20},{8,24},{12,28},{16,0},{20,4},{24,8},{28,12},{1,17},{... | collective-permute-start | bytes 221192 | tf_op jit(solution)/shard_map/ppermute | solution.py:28
  17.3 2.4 %collective-permute-done.4 = s16[288,128]{1,0:T(8,128)(2,1)S(1)} collective-permute-done((s16[288,128]{1,0:T(8,128)(2,1)S(1)}, s16[288,128]{1,0:T(8,128)(2,1)S(1)}, u32[]{:S(2)}, u32[]{:S(2)}) %collective-permute-start.4) | collective-permute-done | bytes 73760 | tf_op jit(solution)/shard_map/ppermute | solution.py:28
  19.7 1.9 %collective-permute-start.5 = (s16[288,128]{1,0:T(8,128)(2,1)S(1)}, s16[288,128]{1,0:T(8,128)(2,1)S(1)}, u32[]{:S(2)}, u32[]{:S(2)}) collective-permute-start(s16[288,128]{1,0:T(8,128)(2,1)S(1)} %add.20.cells_ref), channel_id=1, source_target_pairs={{0,4},{4,0},{8,12},{12,8},{16,20},{20,16},{24,28},{28,24},{1,5},{5... | collective-permute-start | bytes 221192 | tf_op jit(solution)/shard_map/ppermute | solution.py:28
  21.6 1.8 %stage.1 = (bf16[2,16,8,32,128]{4,3,2,1,0:T(8,128)(2,1)S(1)}, f32[3,8,32,128]{3,2,1,0:T(8,128)S(1)}, bf16[264,128]{1,0:T(8,128)(2,1)S(1)}, bf16[264,128]{1,0:T(8,128)(2,1)S(1)}) custom-call(bf16[2,16,8,32,128]{4,3,2,1,0:T(8,128)(2,1)} %f_hbm.1, f32[3,8,32,128]{3,2,1,0:T(8,128)} %winds_hbm.1), custom_call_target="tpu_custom_call" | custom-call | tf_op jit(solution)/shard_map/stage/pallas_call | solution.py:127
  23.4 0.1 collective-permute-start.6
  23.4 1.7 %collective-permute-start.7 = (bf16[264,128]{1,0:T(8,128)(2,1)S(1)}, bf16[264,128]{1,0:T(8,128)(2,1)S(1)}, u32[]{:S(2)}, u32[]{:S(2)}) collective-permute-start(bf16[264,128]{1,0:T(8,128)(2,1)S(1)} %get-tuple-element.17), channel_id=1, source_target_pairs={{0,3},{1,2},{2,1},{3,0},{4,7},{5,6},{6,5},{7,4},{8,11},{9,10},{10,... | collective-permute-start | bytes 202760 | tf_op jit(solution)/shard_map/ppermute | solution.py:28
  25.1 0.0 collective-permute-done.6.inner_ref
  25.1 2.2 %collective-permute-done.7.outer_ref = bf16[264,128]{1,0:T(8,128)(2,1)S(1)} collective-permute-done((bf16[264,128]{1,0:T(8,128)(2,1)S(1)}, bf16[264,128]{1,0:T(8,128)(2,1)S(1)}, u32[]{:S(2)}, u32[]{:S(2)}) %collective-permute-start.7) | collective-permute-done | bytes 67616 | tf_op jit(solution)/shard_map/ppermute | solution.py:28
  27.3 2.5 %advect.2._ = bf16[2,16,8,32,128]{4,3,2,1,0:T(8,128)(2,1)} custom-call(s32[1]{0:T(128)} %bitcast.5.species_ref._, s16[288,128]{1,0:T(8,128)(2,1)S(1)} %add.20.cells_ref, f32[3,8,32,128]{3,2,1,0:T(8,128)S(1)} %get-tuple-element.15.winds_ref, bf16[264,128]{1,0:T(8,128)(2,1)S(1)} %collective-permute-done.6.inner_ref, ...), custom_call_target="tpu_custom_call" | custom-call | tf_op jit(solution)/shard_map/advect/pallas_call | solution.py:243
  29.8 0.0 collective-permute-done.5.cells_ref
  29.8 2.5 %advect.3 = bf16[2,16,8,32,128]{4,3,2,1,0:T(8,128)(2,1)} custom-call(s32[1]{0:T(128)} %bitcast.species_ref, s16[288,128]{1,0:T(8,128)(2,1)S(1)} %collective-permute-done.5.cells_ref, f32[3,8,32,128]{3,2,1,0:T(8,128)S(1)} %get-tuple-element.15.winds_ref, bf16[264,128]{1,0:T(8,128)(2,1)S(1)} %collective-permute-done.6.inner_ref, ...), custom_call_target="tpu_custom_call", output_to_operand_aliasing={{}: (6, {})} | custom-call | tf_op jit(solution)/shard_map/advect/pallas_call | solution.py:243
  (6 shorter events, 0.1 us)
Async XLA Ops:
  1.1 3.9 %collective-permute-start = (s16[32,128]{1,0:T(8,128)(2,1)S(1)}, s16[32,128]{1,0:T(8,128)(2,1)S(1)}, u32[]{:S(2)}, u32[]{:S(2)}) collective-permute-start(s16[32,128]{1,0:T(8,128)(2,1)S(1)} %get-tuple-element.13), channel_id=1, source_target_pairs={{0,3},{1,2},{2,1},{3,0},{4,7},{5,6},{6,5},{7,4},{8,11},{9,10},{10,... | collective-permute-start | bytes 24584 | tf_op jit(solution)/shard_map/ppermute | solution.py:28
  3.6 1.5 %collective-permute-start.1 = (s16[32,128]{1,0:T(8,128)(2,1)S(1)}, s16[32,128]{1,0:T(8,128)(2,1)S(1)}, u32[]{:S(2)}, u32[]{:S(2)}) collective-permute-start(s16[32,128]{1,0:T(8,128)(2,1)S(1)} %get-tuple-element.14), channel_id=1, source_target_pairs={{0,1},{1,0},{2,3},{3,2},{4,5},{5,4},{6,7},{7,6},{8,9},{9,8},{10,11... | collective-permute-start | bytes 24584 | tf_op jit(solution)/shard_map/ppermute | solution.py:28
  5.2 4.8 %collective-permute-start.2 = (s16[288,128]{1,0:T(8,128)(2,1)S(1)}, s16[288,128]{1,0:T(8,128)(2,1)S(1)}, u32[]{:S(2)}, u32[]{:S(2)}) collective-permute-start(s16[288,128]{1,0:T(8,128)(2,1)S(1)} %slice_bitcast_fusion), channel_id=1, source_target_pairs={{0,4},{4,0},{8,12},{12,8},{16,20},{20,16},{24,28},{28,24},{1,5},{5... | collective-permute-start | bytes 221192 | tf_op jit(solution)/shard_map/ppermute | solution.py:28
  9.9 4.4 %collective-permute-start.3 = (s16[288,128]{1,0:T(8,128)(2,1)S(1)}, s16[288,128]{1,0:T(8,128)(2,1)S(1)}, u32[]{:S(2)}, u32[]{:S(2)}) collective-permute-start(s16[288,128]{1,0:T(8,128)(2,1)S(1)} %fusion), channel_id=1, source_target_pairs={{0,8},{4,12},{8,0},{12,4},{16,24},{20,28},{24,16},{28,20},{1,9},{5... | collective-permute-start | bytes 221192 | tf_op jit(solution)/shard_map/ppermute | solution.py:28
  14.4 5.3 %collective-permute-start.4 = (s16[288,128]{1,0:T(8,128)(2,1)S(1)}, s16[288,128]{1,0:T(8,128)(2,1)S(1)}, u32[]{:S(2)}, u32[]{:S(2)}) collective-permute-start(s16[288,128]{1,0:T(8,128)(2,1)S(1)} %add.19), channel_id=1, source_target_pairs={{0,16},{4,20},{8,24},{12,28},{16,0},{20,4},{24,8},{28,12},{1,17},{... | collective-permute-start | bytes 221192 | tf_op jit(solution)/shard_map/ppermute | solution.py:28
  19.7 10.1 %collective-permute-start.5 = (s16[288,128]{1,0:T(8,128)(2,1)S(1)}, s16[288,128]{1,0:T(8,128)(2,1)S(1)}, u32[]{:S(2)}, u32[]{:S(2)}) collective-permute-start(s16[288,128]{1,0:T(8,128)(2,1)S(1)} %add.20.cells_ref), channel_id=1, source_target_pairs={{0,4},{4,0},{8,12},{12,8},{16,20},{20,16},{24,28},{28,24},{1,5},{5... | collective-permute-start | bytes 221192 | tf_op jit(solution)/shard_map/ppermute | solution.py:28
  23.4 1.8 %collective-permute-start.6 = (bf16[264,128]{1,0:T(8,128)(2,1)S(1)}, bf16[264,128]{1,0:T(8,128)(2,1)S(1)}, u32[]{:S(2)}, u32[]{:S(2)}) collective-permute-start(bf16[264,128]{1,0:T(8,128)(2,1)S(1)} %get-tuple-element.16), channel_id=1, source_target_pairs={{0,1},{1,0},{2,3},{3,2},{4,5},{5,4},{6,7},{7,6},{8,9},{9,8},{10,11... | collective-permute-start | bytes 202760 | tf_op jit(solution)/shard_map/ppermute | solution.py:28
  23.4 3.9 %collective-permute-start.7 = (bf16[264,128]{1,0:T(8,128)(2,1)S(1)}, bf16[264,128]{1,0:T(8,128)(2,1)S(1)}, u32[]{:S(2)}, u32[]{:S(2)}) collective-permute-start(bf16[264,128]{1,0:T(8,128)(2,1)S(1)} %get-tuple-element.17), channel_id=1, source_target_pairs={{0,3},{1,2},{2,1},{3,0},{4,7},{5,6},{6,5},{7,4},{8,11},{9,10},{10,... | collective-permute-start | bytes 202760 | tf_op jit(solution)/shard_map/ppermute | solution.py:28

commit v3 on v2

--- a/solution.py
+++ b/solution.py
@@ -1,3 +1,5 @@
+import functools
+
 import jax
 import jax.numpy as jnp
 from jax import lax
@@ -41,8 +43,8 @@
     return jnp.minimum(jnp.maximum(centred, jnp.minimum(before, after)), jnp.maximum(before, after))
 
 
-def coded(values):
-    return (values * SCALE + 0.5).astype(jnp.int32).astype(I16)
+def coded(values, scale):
+    return (values * scale + 0.5).astype(jnp.int32).astype(I16)
 
 
 def decoded(codes):
@@ -61,17 +63,16 @@
     field.wait()
     for k in range(2):
         slot = slots_ref[lax.rem(group + k, 2)]
-        mine = slot // held == group
         at = lax.rem(slot, held)
-        scale = jnp.where(mine, 1.0, 0.0)
+        scale = jnp.where(slot // held == group, SCALE, 0.0)
         for z in range(levels):
-            main_ref[k, pl.ds(z * columns, columns), :] = coded(bulk_ref[at, z] * scale)
+            main_ref[k, pl.ds(z * columns, columns), :] = coded(bulk_ref[at, z], scale)
         for j in range(2):
             low = bulk_ref[at, :, j, :]
             high = bulk_ref[at, :, columns - 2 + j, :]
             rows = pl.ds((2 * k + j) * levels, levels)
-            inner_ref[rows, :] = coded(jnp.where(even, high, low) * scale)
-            outer_ref[rows, :] = coded(jnp.where(even, low, high) * scale)
+            inner_ref[rows, :] = coded(jnp.where(even, high, low), scale)
+            outer_ref[rows, :] = coded(jnp.where(even, low, high), scale)
 
 
 def picked(slots, bulk):
@@ -141,12 +142,18 @@
 
 
 def advect_kernel(
-    species_ref, cells_ref, winds_ref, inner_ref, outer_ref, f_ref, _, out_ref,
-    cell_ext, wind_ext, flux_ext, coef, share_ext, result, sems,
+    last, species_ref, cells_ref, rims_ref, met_ref, winds_ref, inner_ref, outer_ref, f_ref, *refs
 ):
+    if last:
+        before, out_ref, cell_ext, wind_ext, flux_ext, coef, share_ext, result, sems = refs
+    else:
+        result, cell_ext, wind_ext, flux_ext, coef, share_ext = refs
     species, tags, levels, columns, lanes = f_ref.shape
     own = species_ref[0]
     body = pl.ds(PAD, columns)
+    if last:
+        earlier = pltpu.make_async_copy(before, out_ref.at[1 - own], sems.at[tags // TOGETHER])
+        earlier.start()
     tile = lax.axis_index("tile")
     even = tile % 2 == 0
     last_tile = tile == lax.axis_size("tile") - 1
@@ -159,8 +166,19 @@
 
     for z in range(levels):
         cell_ext[z, body, :] = decoded(cells_ref[pl.ds(z * columns, columns), :])
-    for j, row in enumerate((PAD - 2, PAD - 1, PAD + columns, PAD + columns + 1)):
-        cell_ext[:, row, :] = decoded(cells_ref[pl.ds((columns + j) * levels, levels), :])
+    start = rims_ref.shape[0] - 8 * levels
+
+    def rim(row):
+        mine = pl.ds(start + (row + 2 * last) * levels, levels)
+        theirs = pl.ds((row + 2 - 2 * last) * levels, levels)
+        return decoded(rims_ref[mine, :]) + decoded(met_ref[theirs, :])
+
+    for j in range(2):
+        from_inner, from_outer = rim(j), rim(4 + j)
+        low = jnp.where(even, from_outer, from_inner)
+        high = jnp.where(even, from_inner, from_outer)
+        cell_ext[:, PAD - 2 + j, :] = jnp.where(tile == 0, 0.0, low)
+        cell_ext[:, PAD + columns + j, :] = jnp.where(last_tile, 0.0, high)
     wind_ext[:, 0:columns, :] = winds_ref[0]
     wind_ext[:, 0, :] = jnp.where(tile == 0, 0.0, winds_ref[0, :, 0, :])
     above = beyond(pl.ds(species * tags * levels, levels))
@@ -220,7 +238,7 @@
                     total += cs[4] * plane[z - 1]
                 if z < levels - 1:
                     total += cs[5] * plane[z + 1]
-                result[base * TOGETHER + p, z] = total.astype(out_ref.dtype)
+                result[base * TOGETHER + p, z] = total.astype(result.dtype)
         return carry
 
     def stored(j):
@@ -229,70 +247,66 @@
 
     for j in range(tags // TOGETHER):
         lax.fori_loop(j, j + 1, some_tags, 0)
-        stored(j).start()
-    for j in range(tags // TOGETHER):
-        stored(j).wait()
-
-
-def advected(which, cells, winds, from_inner, from_outer, fractions, out):
+        if last:
+            stored(j).start()
+    if last:
+        earlier.wait()
+        for j in range(tags // TOGETHER):
+            stored(j).wait()
+
+
+def advected(which, cells, rims, met, winds, from_inner, from_outer, fractions, before):
     _, tags, levels, columns, lanes = fractions.shape
+    last = before is not None
     whole = pl.BlockSpec(memory_space=pltpu.VMEM)
     scalar = pl.BlockSpec(memory_space=pltpu.SMEM)
-    place = pl.BlockSpec(memory_space=pl.ANY)
-    first = out is None
+    one = (tags, levels, columns, lanes)
+    scratch = [
+        pltpu.VMEM((levels, columns + 24, lanes), F32),
+        pltpu.VMEM((levels, columns + 8, lanes), F32),
+        pltpu.VMEM((levels, columns + 8, lanes), F32),
+        pltpu.VMEM((7, levels, columns, lanes), F32),
+        pltpu.VMEM((TOGETHER, levels, columns + 16, lanes), F32),
+    ]
+    operands = [which, in_vmem(cells), in_vmem(rims), in_vmem(met), winds, in_vmem(from_inner), in_vmem(from_outer), fractions]
+    if last:
+        scratch += [pltpu.VMEM(one, fractions.dtype), pltpu.SemaphoreType.DMA((tags // TOGETHER + 1,))]
+        operands.append(in_vmem(before))
     return pl.pallas_call(
-        advect_kernel,
-        out_shape=jax.ShapeDtypeStruct(fractions.shape, fractions.dtype),
-        in_specs=[scalar, whole, whole, whole, whole, whole, scalar if first else place],
-        out_specs=place,
-        scratch_shapes=[
-            pltpu.VMEM((levels, columns + 24, lanes), F32),
-            pltpu.VMEM((levels, columns + 8, lanes), F32),
-            pltpu.VMEM((levels, columns + 8, lanes), F32),
-            pltpu.VMEM((7, levels, columns, lanes), F32),
-            pltpu.VMEM((TOGETHER, levels, columns + 16, lanes), F32),
-            pltpu.VMEM((tags, levels, columns, lanes), fractions.dtype),
-            pltpu.SemaphoreType.DMA((tags // TOGETHER,)),
-        ],
-        input_output_aliases={} if first else {6: 0},
+        functools.partial(advect_kernel, last),
+        out_shape=jax.ShapeDtypeStruct(fractions.shape if last else one, fractions.dtype),
+        in_specs=[scalar] + [whole] * (len(operands) - 1),
+        out_specs=pl.BlockSpec(memory_space=pl.ANY) if last else whole,
+        scratch_shapes=scratch,
         compiler_params=LIMIT,
         name="advect",
-    )(which, in_vmem(cells), winds, in_vmem(from_inner), in_vmem(from_outer), fractions, which if first else out)
+    )(*operands)
 
 
 def shards(species_slot, bulk, winds, fractions):
-    _, levels, _, lanes = bulk.shape
-    group, tile = lax.axis_index("tag"), lax.axis_index("tile")
-    groups, tiles = lax.axis_size("tag"), lax.axis_size("tile")
-    even = tile % 2 == 0
+    _, levels, columns, _ = bulk.shape
+    group, groups = lax.axis_index("tag"), lax.axis_size("tag")
+    size = levels * columns
 
     main, inner_edge, outer_edge = picked(species_slot, bulk)
-    from_outer = paired(outer_edge, "tile", outer)
-    from_inner = paired(inner_edge, "tile", inner)
-    low = jnp.where(even, from_outer, from_inner).reshape(2, 2 * levels, lanes)
-    high = jnp.where(even, from_inner, from_outer).reshape(2, 2 * levels, lanes)
-    low = jnp.where(tile == 0, jnp.zeros_like(low), low)
-    high = jnp.where(tile == tiles - 1, jnp.zeros_like(high), high)
-    rows = jnp.concatenate([main, low, high], axis=1)
-
+    came = paired(main[1], "tag", inner)
+    rim_outer = paired(outer_edge, "tile", outer)
+    rim_inner = paired(inner_edge, "tile", inner)
     fractions, winds, inner_rows, outer_rows = staged(fractions, winds)
-    got_inner = paired(inner_rows, "tile", inner)
-    got_outer = paired(outer_rows, "tile", outer)
-
-    crossed = paired(rows[1], "tag", inner)
-    own = rows[0] + crossed
+    own = jnp.concatenate([main[0] + came, rim_inner, rim_outer])
     bit = 2
     while bit < groups:
         came = paired(own, "tag", lambda i, count: i ^ bit)
         own = own + came
         bit *= 2
-    other = paired(own, "tag", inner)
-
-    out = None
-    for k, cells in enumerate((own, other)):
-        which = lax.rem(group + k, 2)[None]
-        out = advected(which, cells, winds, got_inner, got_outer, fractions, out)
-    return out
+    got_inner = paired(inner_rows, "tile", inner)
+    got_outer = paired(outer_rows, "tile", outer)
+    met = paired(own[size:], "tag", inner)
+    other = paired(own[:size], "tag", inner)
+
+    which = lax.rem(group, 2)[None]
+    done = advected(which, own, own, met, winds, got_inner, got_outer, fractions, None)
+    return advected(1 - which, other, own, met, winds, got_inner, got_outer, fractions, done)
 
 
 def solution(mesh):

time: 32.4 us -> 27.9 us (0.86)
  waiting for transfers between devices: 10.4 us -> 7.83 us
  starting transfers between devices: 13.9 us -> 12.7 us
  Pallas kernels: 7.8 us -> 7.02 us
    ppermute x8 -> x9, waiting for transfers between devices: 10.4 us -> 7.83 us  [paired(): lax.ppermute(value, axis, [(i, flip(i, count)) for i in range(count)])]
    ppermute x8 -> x9, starting transfers between devices: 13.9 us -> 12.7 us  [paired(): lax.ppermute(value, axis, [(i, flip(i, count)) for i in range(count)])]
    pallas_call x2, Pallas kernels: 4.94 us -> 4.18 us  [advected(): pl.pallas_call(functools.partial(advect_kernel, last), out_shape=jax.Shap...]
  transfers between devices with their start and end apart: 8 -> 9, of which waited for: 6 -> 5; matrix products, arithmetic and copies ran while one was open for 0% -> 0% of each run, Pallas kernels for 13% -> 13%
where the time goes in v3:
time: 27.9 us; the launch traced here: 27.7 us
  starting transfers between devices  12.7 us (46%)
  waiting for transfers between devices  7.83 us (28%)
  Pallas kernels  7.02 us (25%)
    ppermute x9, starting transfers between devices, paired(): lax.ppermute(value, axis, [(i, flip(i, count)) for i in range(count)])  12.7 us
    ppermute x9, waiting for transfers between devices, paired(): lax.ppermute(value, axis, [(i, flip(i, count)) for i in range(count)])  7.83 us
    pallas_call x2, Pallas kernels, advected(): pl.pallas_call(functools.partial(advect_kernel, last), out_shape=jax.Shap...  4.18 us
    pallas_call x1, Pallas kernels, staged(): pl.pallas_call(stage_kernel, out_shape=(jax.ShapeDtypeStruct(fractions.sh...  1.76 us
    pallas_call x1, Pallas kernels, picked(): pl.pallas_call(pick_kernel, out_shape=(jax.ShapeDtypeStruct((2, levels *...  1.09 us
  transfers between devices with their start and end apart: 9, of which 5 were waited for; matrix products, arithmetic and copies ran while one was open for 0% of the time, Pallas kernels for 13%

profile of v3, /device:TPU:0, one launch (start us, length us, event | category | flops | bytes accessed | tf_op | source)
XLA Modules:
  0.0 27.7 jit_solution(7679761093991615207)
XLA Ops:
  0.0 1.1 %pick.1 = (s16[2,256,128]{2,1,0:T(8,128)(2,1)S(1)}, s16[32,128]{1,0:T(8,128)(2,1)S(1)}, s16[32,128]{1,0:T(8,128)(2,1)S(1)}) custom-call(s32[16]{0:T(128)} %slots_hbm.1, f32[2,8,32,128]{3,2,1,0:T(8,128)} %bulk_hbm.1), custom_call_target="tpu_custom_call" | custom-call | tf_op jit(solution)/shard_map/pick/pallas_call | solution.py:83
  1.1 3.0 %collective-permute-start = (s16[256,128]{1,0:T(8,128)(2,1)S(1)}, s16[256,128]{1,0:T(8,128)(2,1)S(1)}, u32[]{:S(2)}, u32[]{:S(2)}) collective-permute-start(s16[256,128]{1,0:T(8,128)(2,1)S(1)} %slice_bitcast_fusion), channel_id=1, source_target_pairs={{0,4},{4,0},{8,12},{12,8},{16,20},{20,16},{24,28},{28,24},{1,5},{5... | collective-permute-start | bytes 196616 | tf_op jit(solution)/shard_map/ppermute | solution.py:30
  4.1 0.0 collective-permute-start.1
  4.1 1.6 %collective-permute-start.2 = (s16[32,128]{1,0:T(8,128)(2,1)S(1)}, s16[32,128]{1,0:T(8,128)(2,1)S(1)}, u32[]{:S(2)}, u32[]{:S(2)}) collective-permute-start(s16[32,128]{1,0:T(8,128)(2,1)S(1)} %get-tuple-element.14), channel_id=1, source_target_pairs={{0,3},{1,2},{2,1},{3,0},{4,7},{5,6},{6,5},{7,4},{8,11},{9,10},{10,... | collective-permute-start | bytes 24584 | tf_op jit(solution)/shard_map/ppermute | solution.py:30
  5.8 0.6 %collective-permute-done = s16[256,128]{1,0:T(8,128)(2,1)S(1)} collective-permute-done((s16[256,128]{1,0:T(8,128)(2,1)S(1)}, s16[256,128]{1,0:T(8,128)(2,1)S(1)}, u32[]{:S(2)}, u32[]{:S(2)}) %collective-permute-start) | collective-permute-done | bytes 65568 | tf_op jit(solution)/shard_map/ppermute | solution.py:30
  6.4 0.0 collective-permute-done.1
  6.4 0.8 %collective-permute-done.2 = s16[32,128]{1,0:T(8,128)(2,1)S(1)} collective-permute-done((s16[32,128]{1,0:T(8,128)(2,1)S(1)}, s16[32,128]{1,0:T(8,128)(2,1)S(1)}, u32[]{:S(2)}, u32[]{:S(2)}) %collective-permute-start.2) | collective-permute-done | bytes 8224 | tf_op jit(solution)/shard_map/ppermute | solution.py:30
  7.2 1.6 %collective-permute-start.3 = (s16[320,128]{1,0:T(8,128)(2,1)S(1)}, s16[320,128]{1,0:T(8,128)(2,1)S(1)}, u32[]{:S(2)}, u32[]{:S(2)}) collective-permute-start(s16[320,128]{1,0:T(8,128)(2,1)S(1)} %pad_add_fusion), channel_id=1, source_target_pairs={{0,8},{4,12},{8,0},{12,4},{16,24},{20,28},{24,16},{28,20},{1,9},{5... | collective-permute-start | bytes 245768 | tf_op jit(solution)/shard_map/ppermute | solution.py:30
  8.8 3.3 %collective-permute-done.3 = s16[320,128]{1,0:T(8,128)(2,1)S(1)} collective-permute-done((s16[320,128]{1,0:T(8,128)(2,1)S(1)}, s16[320,128]{1,0:T(8,128)(2,1)S(1)}, u32[]{:S(2)}, u32[]{:S(2)}) %collective-permute-start.3) | collective-permute-done | bytes 81952 | tf_op jit(solution)/shard_map/ppermute | solution.py:30
  12.1 2.7 %collective-permute-start.4 = (s16[320,128]{1,0:T(8,128)(2,1)S(1)}, s16[320,128]{1,0:T(8,128)(2,1)S(1)}, u32[]{:S(2)}, u32[]{:S(2)}) collective-permute-start(s16[320,128]{1,0:T(8,128)(2,1)S(1)} %fusion), channel_id=1, source_target_pairs={{0,16},{4,20},{8,24},{12,28},{16,0},{20,4},{24,8},{28,12},{1,17},{... | collective-permute-start | bytes 245768 | tf_op jit(solution)/shard_map/ppermute | solution.py:30
  14.8 1.8 %stage.1 = (bf16[2,16,8,32,128]{4,3,2,1,0:T(8,128)(2,1)S(1)}, f32[3,8,32,128]{3,2,1,0:T(8,128)S(1)}, bf16[264,128]{1,0:T(8,128)(2,1)S(1)}, bf16[264,128]{1,0:T(8,128)(2,1)S(1)}) custom-call(bf16[2,16,8,32,128]{4,3,2,1,0:T(8,128)(2,1)} %f_hbm.1, f32[3,8,32,128]{3,2,1,0:T(8,128)} %winds_hbm.1), custom_call_target="tpu_custom_call" | custom-call | tf_op jit(solution)/shard_map/stage/pallas_call | solution.py:128
  16.5 0.1 collective-permute-start.7
  16.6 1.6 %collective-permute-start.8 = (bf16[264,128]{1,0:T(8,128)(2,1)S(1)}, bf16[264,128]{1,0:T(8,128)(2,1)S(1)}, u32[]{:S(2)}, u32[]{:S(2)}) collective-permute-start(bf16[264,128]{1,0:T(8,128)(2,1)S(1)} %get-tuple-element.17), channel_id=1, source_target_pairs={{0,3},{1,2},{2,1},{3,0},{4,7},{5,6},{6,5},{7,4},{8,11},{9,10},{10,... | collective-permute-start | bytes 202760 | tf_op jit(solution)/shard_map/ppermute | solution.py:30
  18.2 0.7 %collective-permute-done.4 = s16[320,128]{1,0:T(8,128)(2,1)S(1)} collective-permute-done((s16[320,128]{1,0:T(8,128)(2,1)S(1)}, s16[320,128]{1,0:T(8,128)(2,1)S(1)}, u32[]{:S(2)}, u32[]{:S(2)}) %collective-permute-start.4) | collective-permute-done | bytes 81952 | tf_op jit(solution)/shard_map/ppermute | solution.py:30
  19.0 0.2 collective-permute-start.5
  19.2 1.9 %collective-permute-start.6 = (s16[64,128]{1,0:T(8,128)(2,1)S(1)}, s16[64,128]{1,0:T(8,128)(2,1)S(1)}, u32[]{:S(2)}, u32[]{:S(2)}) collective-permute-start(s16[64,128]{1,0:T(8,128)(2,1)S(1)} %slice.17), channel_id=1, source_target_pairs={{0,4},{4,0},{8,12},{12,8},{16,20},{20,16},{24,28},{28,24},{1,5},{5... | collective-permute-start | bytes 49160 | tf_op jit(solution)/shard_map/ppermute | solution.py:30
  21.1 0.0 collective-permute-done.7.inner_ref
  21.1 0.0 collective-permute-done.8.outer_ref
  21.1 2.4 %collective-permute-done.6.met_ref = s16[64,128]{1,0:T(8,128)(2,1)S(1)} collective-permute-done((s16[64,128]{1,0:T(8,128)(2,1)S(1)}, s16[64,128]{1,0:T(8,128)(2,1)S(1)}, u32[]{:S(2)}, u32[]{:S(2)}) %collective-permute-start.6) | collective-permute-done | bytes 16416 | tf_op jit(solution)/shard_map/ppermute | solution.py:30
  23.5 1.7 %advect.2.refs_0_ = bf16[16,8,32,128]{3,2,1,0:T(8,128)(2,1)S(1)} custom-call(s32[1]{0:T(128)} %bitcast.species_ref, s16[320,128]{1,0:T(8,128)(2,1)S(1)} %add.11.cells_ref.rims_ref, s16[320,128]{1,0:T(8,128)(2,1)S(1)} %add.11.cells_ref.rims_ref, s16[64,128]{1,0:T(8,128)(2,1)S(1)} %collective-permute-done.6.met_ref, ...), custom_call_target="tpu_custom_call" | custom-call | tf_op jit(solution)/shard_map/advect/pallas_call | solution.py:275
  25.2 0.0 collective-permute-done.5.cells_ref
  25.2 2.5 %advect.3 = bf16[2,16,8,32,128]{4,3,2,1,0:T(8,128)(2,1)} custom-call(s32[1]{0:T(128)S(6)} %sub.3.species_ref, s16[256,128]{1,0:T(8,128)(2,1)S(1)} %collective-permute-done.5.cells_ref, s16[320,128]{1,0:T(8,128)(2,1)S(1)} %add.11.cells_ref.rims_ref, s16[64,128]{1,0:T(8,128)(2,1)S(1)} %collective-permute-done.6.met_ref, ...), custom_call_target="tpu_custom_call" | custom-call | tf_op jit(solution)/shard_map/advect/pallas_call | solution.py:275
  (7 shorter events, 0.1 us)
Async XLA Ops:
  1.1 5.3 %collective-permute-start = (s16[256,128]{1,0:T(8,128)(2,1)S(1)}, s16[256,128]{1,0:T(8,128)(2,1)S(1)}, u32[]{:S(2)}, u32[]{:S(2)}) collective-permute-start(s16[256,128]{1,0:T(8,128)(2,1)S(1)} %slice_bitcast_fusion), channel_id=1, source_target_pairs={{0,4},{4,0},{8,12},{12,8},{16,20},{20,16},{24,28},{28,24},{1,5},{5... | collective-permute-start | bytes 196616 | tf_op jit(solution)/shard_map/ppermute | solution.py:30
  4.1 2.3 %collective-permute-start.1 = (s16[32,128]{1,0:T(8,128)(2,1)S(1)}, s16[32,128]{1,0:T(8,128)(2,1)S(1)}, u32[]{:S(2)}, u32[]{:S(2)}) collective-permute-start(s16[32,128]{1,0:T(8,128)(2,1)S(1)} %get-tuple-element.13), channel_id=1, source_target_pairs={{0,1},{1,0},{2,3},{3,2},{4,5},{5,4},{6,7},{7,6},{8,9},{9,8},{10,11... | collective-permute-start | bytes 24584 | tf_op jit(solution)/shard_map/ppermute | solution.py:30
  4.1 3.1 %collective-permute-start.2 = (s16[32,128]{1,0:T(8,128)(2,1)S(1)}, s16[32,128]{1,0:T(8,128)(2,1)S(1)}, u32[]{:S(2)}, u32[]{:S(2)}) collective-permute-start(s16[32,128]{1,0:T(8,128)(2,1)S(1)} %get-tuple-element.14), channel_id=1, source_target_pairs={{0,3},{1,2},{2,1},{3,0},{4,7},{5,6},{6,5},{7,4},{8,11},{9,10},{10,... | collective-permute-start | bytes 24584 | tf_op jit(solution)/shard_map/ppermute | solution.py:30
  7.2 4.9 %collective-permute-start.3 = (s16[320,128]{1,0:T(8,128)(2,1)S(1)}, s16[320,128]{1,0:T(8,128)(2,1)S(1)}, u32[]{:S(2)}, u32[]{:S(2)}) collective-permute-start(s16[320,128]{1,0:T(8,128)(2,1)S(1)} %pad_add_fusion), channel_id=1, source_target_pairs={{0,8},{4,12},{8,0},{12,4},{16,24},{20,28},{24,16},{28,20},{1,9},{5... | collective-permute-start | bytes 245768 | tf_op jit(solution)/shard_map/ppermute | solution.py:30
  12.1 6.9 %collective-permute-start.4 = (s16[320,128]{1,0:T(8,128)(2,1)S(1)}, s16[320,128]{1,0:T(8,128)(2,1)S(1)}, u32[]{:S(2)}, u32[]{:S(2)}) collective-permute-start(s16[320,128]{1,0:T(8,128)(2,1)S(1)} %fusion), channel_id=1, source_target_pairs={{0,16},{4,20},{8,24},{12,28},{16,0},{20,4},{24,8},{28,12},{1,17},{... | collective-permute-start | bytes 245768 | tf_op jit(solution)/shard_map/ppermute | solution.py:30
  16.5 4.6 %collective-permute-start.7 = (bf16[264,128]{1,0:T(8,128)(2,1)S(1)}, bf16[264,128]{1,0:T(8,128)(2,1)S(1)}, u32[]{:S(2)}, u32[]{:S(2)}) collective-permute-start(bf16[264,128]{1,0:T(8,128)(2,1)S(1)} %get-tuple-element.16), channel_id=1, source_target_pairs={{0,1},{1,0},{2,3},{3,2},{4,5},{5,4},{6,7},{7,6},{8,9},{9,8},{10,11... | collective-permute-start | bytes 202760 | tf_op jit(solution)/shard_map/ppermute | solution.py:30
  16.6 4.5 %collective-permute-start.8 = (bf16[264,128]{1,0:T(8,128)(2,1)S(1)}, bf16[264,128]{1,0:T(8,128)(2,1)S(1)}, u32[]{:S(2)}, u32[]{:S(2)}) collective-permute-start(bf16[264,128]{1,0:T(8,128)(2,1)S(1)} %get-tuple-element.17), channel_id=1, source_target_pairs={{0,3},{1,2},{2,1},{3,0},{4,7},{5,6},{6,5},{7,4},{8,11},{9,10},{10,... | collective-permute-start | bytes 202760 | tf_op jit(solution)/shard_map/ppermute | solution.py:30
  19.0 6.2 %collective-permute-start.5 = (s16[256,128]{1,0:T(8,128)(2,1)S(1)}, s16[256,128]{1,0:T(8,128)(2,1)S(1)}, u32[]{:S(2)}, u32[]{:S(2)}) collective-permute-start(s16[256,128]{1,0:T(8,128)(2,1)S(1)} %slice.16), channel_id=1, source_target_pairs={{0,4},{4,0},{8,12},{12,8},{16,20},{20,16},{24,28},{28,24},{1,5},{5... | collective-permute-start | bytes 196616 | tf_op jit(solution)/shard_map/ppermute | solution.py:30
  19.2 4.3 %collective-permute-start.6 = (s16[64,128]{1,0:T(8,128)(2,1)S(1)}, s16[64,128]{1,0:T(8,128)(2,1)S(1)}, u32[]{:S(2)}, u32[]{:S(2)}) collective-permute-start(s16[64,128]{1,0:T(8,128)(2,1)S(1)} %slice.17), channel_id=1, source_target_pairs={{0,4},{4,0},{8,12},{12,8},{16,20},{20,16},{24,28},{28,24},{1,5},{5... | collective-permute-start | bytes 49160 | tf_op jit(solution)/shard_map/ppermute | solution.py:30
